TPU v7x, 128 devices: a whole 4x4x4 slice. The times are simulated.
128 devices in a mesh: spin: 8 (over y, core), fock: 16 (over x, z).
Axes of the slice: x: 4, y: 4, z: 4, core: 2. Of those that a mesh axis runs over, the one named last changes fastest.
Arguments:
- amplitudes: float32 [2, 8192, 8192], P(None, 'spin', 'fock'), may hold values from -6 to 6
- cutoffs: int32 [8192], P('spin'), may hold values from 256 to 512
- coupling_first: float32 [13], replicated, may hold values from 0.05 to 0.5
- coupling_second: float32 [13], replicated, may hold values from 0.2 to 2
- frozen_coupling: float32 [16], replicated, may hold values from 1 to 4
- frozen_bits: int32 [16], replicated, may hold values from 0 to 1, as said below
- drive_bits: int32 [13], replicated, may hold values 0 or 1
- angles: float32 [13], replicated, may hold values from 0.3 to 1.3
Outputs:
- evolved: float32 [2, 8192, 8192], P(None, 'spin', 'fock')
Inputs may be any that keep to these rules, and one draw needn't show every extreme that they name: `cutoffs`: highest level plus one of the first mode that the ladder couples in each spin configuration. `frozen_bits`: between one and four frozen spins have bit 1, the others bit 0.
All inputs are finite; a program needn't handle non-finite values.
Results may differ from a plain program's by a relative error of at most 0.0003.
Values sent between devices are 32-bit elements; how exact they have to be, the bound alone decides.
A program may use at most 192 MiB of HBM per device.

v0:
```python
import math

import jax
import jax.numpy as jnp
from jax import lax
from jax.sharding import PartitionSpec as P

SPINS = 13
FA = 512
FB = 16
DEGREE = 16


evolve_time = 12.0
diagonal_first = 0.06
diagonal_second = 0.04
ladder_first = 0.35
ladder_second = 0.1


def in_blocks(value, dim, length):
    lengths = value.shape
    parts = value.reshape(*lengths[:dim], length, lengths[dim] // length, *lengths[dim + 1 :])
    return jnp.moveaxis(parts, dim, 0)


def cut_rows(length, count):
    unit = 8 if length >= 8 * count else 1
    return [length // unit * k // count * unit for k in range(1, count)]


def in_order(parts, dim):
    parts = jnp.moveaxis(parts, 0, dim)
    lengths = parts.shape
    return parts.reshape(*lengths[:dim], lengths[dim] * lengths[dim + 1], *lengths[dim + 2 :])


def several_exchanges(value, axis, pieces, split_dim, concat_dim):
    parts = in_blocks(value, split_dim, lax.axis_size(axis))
    widest = max(range(1, max(2, parts.ndim - 1)), key=lambda d: parts.shape[d])
    done = []
    for slab in jnp.split(parts, cut_rows(parts.shape[widest], pieces), axis=widest):
        if slab.size:
            done.append(lax.all_to_all(slab, axis, split_axis=0, concat_axis=0, tiled=True))
    return in_order(jnp.concatenate(done, axis=widest), concat_dim)


def bessel_first(term_order, argument):
    running = 0.0
    addend = (argument / 2.0) ** term_order / math.factorial(term_order)
    for serial in range(80):
        running = running + addend
        addend = addend * -(argument * argument / 4.0) / ((serial + 1) * (serial + 1 + term_order))
    return running


def coefficient_table(term_count):
    real_table = []
    imag_table = []
    for term_order in range(term_count + 1):
        magnitude = (1.0 if term_order == 0 else 2.0) * bessel_first(term_order, evolve_time)
        quarter = term_order % 4
        real_table.append(magnitude if quarter == 0 else -magnitude if quarter == 2 else 0.0)
        imag_table.append(-magnitude if quarter == 1 else magnitude if quarter == 3 else 0.0)
    return (real_table, imag_table)


def spin_strengths(config_index, coupling_first, coupling_second, frozen_coupling, frozen_bits):
    spin_bits = config_index[:, None] >> jnp.arange(SPINS, dtype=jnp.int32)[None, :] & 1
    spin_signs = (1 - 2 * spin_bits).astype(jnp.float32)
    frozen_signs = (1 - 2 * frozen_bits).astype(jnp.float32)
    frozen_part = jnp.sum(frozen_coupling * frozen_signs)
    total_first = jnp.sum(coupling_first) + jnp.sum(frozen_coupling)
    strength_first = (
        ladder_first
        * (jnp.sum(spin_signs * coupling_first[None, :], axis=1) + frozen_part)
        / total_first
    )
    strength_second = (
        ladder_second
        * jnp.sum(spin_signs * coupling_second[None, :], axis=1)
        / jnp.sum(coupling_second)
    )
    return (strength_first, strength_second)


def apply_hamiltonian(padded, strength_first, strength_second, cutoff_rows):
    column_count = padded.shape[2] - 2 * FB
    center = padded[:, :, FB : FB + column_count]
    lower_level = padded[:, :, :column_count]
    upper_level = padded[:, :, 2 * FB :]
    column = lax.broadcasted_iota(jnp.int32, (1, column_count), 1)
    level_index = column // FB
    sub_index = column % FB
    cutoff = cutoff_rows[:, None]
    level_float = level_index.astype(jnp.float32)
    sub_float = sub_index.astype(jnp.float32)
    mode_low = jnp.where(
        (level_index >= 1) & (level_index < cutoff),
        jnp.sqrt(jnp.maximum(level_float, 0.0) / FA),
        0.0,
    )
    mode_high = jnp.where(
        (level_index + 1 >= 1) & (level_index + 1 < cutoff),
        jnp.sqrt(jnp.maximum(level_float + 1.0, 0.0) / FA),
        0.0,
    )
    sub_low = jnp.sqrt(sub_float / FB)
    sub_high = jnp.where(sub_index + 1 < FB, jnp.sqrt((sub_float + 1.0) / FB), 0.0)
    diagonal = diagonal_first * (2.0 * level_float / (FA - 1) - 1.0) + diagonal_second * (
        2.0 * sub_float / (FB - 1) - 1.0
    )
    previous_sub = jnp.pad(center[:, :, :-1], ((0, 0), (0, 0), (1, 0)))
    next_sub = jnp.pad(center[:, :, 1:], ((0, 0), (0, 0), (0, 1)))
    first_term = strength_first[None, :, None] * (
        mode_low[None] * lower_level + mode_high[None] * upper_level
    )
    second_term = strength_second[None, :, None] * (
        sub_low[None] * previous_sub + sub_high[None] * next_sub
    )
    return diagonal[None] * center + first_term + second_term


def weighted_term(term_vector, real_weight, imag_weight):
    rotated = jnp.stack([-term_vector[1], term_vector[0]])
    return real_weight * term_vector + imag_weight * rotated


def chebyshev_series(vector, apply_operator, term_count):
    real_table, imag_table = coefficient_table(term_count)
    real_weights = jnp.asarray(real_table, dtype=jnp.float32)
    imag_weights = jnp.asarray(imag_table, dtype=jnp.float32)
    current = apply_operator(vector)
    running = weighted_term(vector, real_weights[0], imag_weights[0]) + weighted_term(
        current, real_weights[1], imag_weights[1]
    )

    def advance(term_index, loop_state):
        previous, present, total = loop_state
        following = 2.0 * apply_operator(present) - previous
        total = total + weighted_term(following, real_weights[term_index], imag_weights[term_index])
        return (present, following, total)

    loop_state = lax.fori_loop(2, term_count + 1, advance, (vector, current, running))
    return loop_state[2]


def partner_term(own_part, partner, cosine, sine_value, phase_bit, side_sign):
    keep_part = 1.0 - phase_bit
    real_part = cosine * own_part[0] + sine_value * (
        side_sign * phase_bit * partner[0] + keep_part * partner[1]
    )
    imag_part = cosine * own_part[1] + sine_value * (
        side_sign * phase_bit * partner[1] - keep_part * partner[0]
    )
    return jnp.stack([real_part, imag_part])


def rotate_bits(vector, bit_list, angles, drive_bits):
    cosines = jnp.cos(angles)
    sine_values = jnp.sin(angles)
    phases = drive_bits.astype(jnp.float32)
    for spin_slot, bit_number in bit_list:
        config_total = vector.shape[1]
        lower_size = 1 << bit_number
        shaped = vector.reshape(2, config_total // (2 * lower_size), 2, lower_size, vector.shape[2])
        lower_half = shaped[:, :, 0]
        upper_half = shaped[:, :, 1]
        new_lower = partner_term(
            lower_half,
            upper_half,
            cosines[spin_slot],
            sine_values[spin_slot],
            phases[spin_slot],
            -1.0,
        )
        new_upper = partner_term(
            upper_half,
            lower_half,
            cosines[spin_slot],
            sine_values[spin_slot],
            phases[spin_slot],
            1.0,
        )
        vector = jnp.stack([new_lower, new_upper], axis=2).reshape(vector.shape)
    return vector


def per_device(
    amplitudes,
    cutoffs,
    coupling_first,
    coupling_second,
    frozen_coupling,
    frozen_bits,
    drive_bits,
    angles,
):
    local_configs = amplitudes.shape[1]
    column_count = amplitudes.shape[2]
    spin_place = lax.axis_index("spin")
    fock_place = lax.axis_index("fock")
    config_index = spin_place * local_configs + lax.iota(jnp.int32, local_configs)
    strength_first, strength_second = spin_strengths(
        config_index, coupling_first, coupling_second, frozen_coupling, frozen_bits
    )
    share = local_configs // lax.axis_size("fock")
    offset = fock_place * share
    full_levels = several_exchanges(amplitudes, "fock", 2, 1, 2)
    share_first = lax.dynamic_slice_in_dim(strength_first, offset, share)
    share_second = lax.dynamic_slice_in_dim(strength_second, offset, share)
    share_cutoffs = lax.dynamic_slice_in_dim(cutoffs, offset, share)

    def apply_operator(field):
        padded = jnp.pad(field, ((0, 0), (0, 0), (FB, FB)))
        return apply_hamiltonian(padded, share_first, share_second, share_cutoffs)

    evolved_share = chebyshev_series(full_levels, apply_operator, DEGREE)
    propagated = several_exchanges(evolved_share, "fock", 2, 2, 1)
    local_bits = local_configs.bit_length() - 1
    spin_count = lax.axis_size("spin")
    split_bits = spin_count.bit_length() - 1
    result = rotate_bits(
        propagated, [(slot, slot) for slot in range(local_bits)], angles, drive_bits
    )
    rest = local_configs // spin_count
    rest_bits = rest.bit_length() - 1
    grouped = result.reshape(2, 1, spin_count, rest, column_count)
    moved = lax.all_to_all(grouped, "spin", split_axis=2, concat_axis=1, tiled=True)
    moved = rotate_bits(
        moved.reshape(2, spin_count * rest, column_count),
        [(local_bits + bit_number, rest_bits + bit_number) for bit_number in range(split_bits)],
        angles,
        drive_bits,
    )
    returned = lax.all_to_all(
        moved.reshape(2, spin_count, 1, rest, column_count),
        "spin",
        split_axis=1,
        concat_axis=2,
        tiled=True,
    )
    return returned.reshape(2, local_configs, column_count)


def solution(mesh):
    placed = (P(None, "spin", "fock"), P("spin"), P(), P(), P(), P(), P(), P())
    return jax.shard_map(
        per_device, mesh=mesh, in_specs=placed, out_specs=P(None, "spin", "fock"), check_vma=False
    )
```

profile of v0, /device:TPU:1, one launch (start us, length us, event | category | flops | bytes accessed | tf_op | source)
XLA Modules:
  0.0 873.6 jit_solution(2232515287772725209)
XLA Ops:
  0.0 4.2 fusion.133
  5.8 8.4 all-to-all-start
  23.0 19.4 %all-to-all-done = f32[16,2,32,512]{3,2,1,0:T(8,128)S(1)} async-done(((f32[16,2,32,512]{3,2,1,0:T(8,128)}), f32[16,2,32,512]{3,2,1,0:T(8,128)S(1)}, u32[]{:S(2)}, u32[]{:S(2)}) %all-to-all-start) | async-done | bytes 2097184 | tf_op jit(solution)/shard_map/all_to_all | solution.py:44
  42.4 4.4 all-to-all-start.1
  49.6 22.7 %all-to-all-done.1 = f32[16,2,32,512]{3,2,1,0:T(8,128)} async-done(((f32[16,2,32,512]{3,2,1,0:T(8,128)}), f32[16,2,32,512]{3,2,1,0:T(8,128)}, u32[]{:S(2)}, u32[]{:S(2)}) %all-to-all-start.1) | async-done | bytes 2097184 | tf_op jit(solution)/shard_map/all_to_all | solution.py:44
  77.1 5.2 multiply_add_fusion
  87.3 453.5 %while.22 = (s32[]{:T(128)}, f32[2,64,8192]{2,1,0:T(8,128)}, f32[2,64,8192]{2,1,0:T(8,128)}, f32[2,64,8192]{2,1,0:T(8,128)}, f32[64]{0:T(128)S(1)}, /*index=5*/s...) while((s32[]{:T(128)}, f32[2,64,8192]{2,1,0:T(8,128)}, ...), condition=%wide.region_7.8_spmd.clone, body=%wide.region_6.7_spmd.sunk.clone.sunk | while | flops 23101440 | bytes 172456048 | solution.py:144
  94.0 5.5 multiply_subtract_fusion.3
  103.4 8.6 fusion.145
  124.2 5.5 multiply_subtract_fusion.3
  133.6 8.6 fusion.145
  154.4 5.5 multiply_subtract_fusion.3
  163.9 8.6 fusion.145
  184.6 5.5 multiply_subtract_fusion.3
  194.1 8.6 fusion.145
  214.8 5.5 multiply_subtract_fusion.3
  224.3 8.6 fusion.145
  245.1 5.5 multiply_subtract_fusion.3
  254.5 8.6 fusion.145
  275.3 5.5 multiply_subtract_fusion.3
  284.7 8.6 fusion.145
  305.5 5.5 multiply_subtract_fusion.3
  314.9 8.6 fusion.145
  335.7 5.5 multiply_subtract_fusion.3
  345.1 8.6 fusion.145
  365.9 5.5 multiply_subtract_fusion.3
  375.4 8.6 fusion.145
  396.1 5.5 multiply_subtract_fusion.3
  405.6 8.6 fusion.145
  426.3 5.5 multiply_subtract_fusion.3
  435.8 8.6 fusion.145
  456.6 5.5 multiply_subtract_fusion.3
  466.0 8.6 fusion.145
  486.8 5.5 multiply_subtract_fusion.3
  496.2 8.6 fusion.145
  517.0 5.5 multiply_subtract_fusion.3
  526.4 8.6 fusion.145
  540.7 5.4 copy.832
  552.2 30.6 %all_to_all.38 = f32[16,2,32,512]{3,1,2,0:T(2,128)S(1)} all-to-all(f32[16,2,32,512]{3,1,2,0:T(2,128)S(1)} %get-tuple-element.459), channel_id=1, replica_groups=mesh['spin'=8,'fock'=16] {'fock'}, dimensions={0} | all-to-all | bytes 4194304 | tf_op jit(solution)/shard_map/all_to_all | solution.py:44
  582.8 4.5 all-to-all-start.3
  601.9 8.7 all-to-all-done.3
  614.3 11.8 %fusion.130 = (f32[1,512,1,1,512]{4,0,2,1,3:T(1,128)S(1)}, f32[1,512,1,1,512]{4,0,2,1,3:T(1,128)S(1)}, f32[1,512,1,1,512]{4,0,2,1,3:T(1,128)S(1)}, f32[1,512,1,1,512]{4,0,2,1,3:T(1,128)S(1)}) fusion(f32[2,512,2,1,512]{4,0,2,1,3:T(2,128)S(1)} %bitcast.718), kind=kLoop, calls=%fused_computation.288 | loop fusion | bytes 8388608 | tf_op jit(solution)/shard_map/slice | solution.py:151
  653.4 9.7 %add_bitcast_fusion.16 = (f32[1,128,4,512]{3,0,2,1:T(1,128)S(1)}, f32[1,128,4,512]{3,0,2,1:T(1,128)S(1)}, f32[1,128,4,512]{3,0,2,1:T(1,128)S(1)}, f32[1,128,4,512]{3,0,2,1:T(1,128)S(1)}) fusion(f32[]{:T(128)S(6)} %sub.436, f32[]{:T(128)S(6)} %mul.3391, f32[]{:T(128)} %bitcast.31, f32[]{:T(128)} %bitcast.10, f32[2,128,2,4,512]{4,0,3,2,1:T(2,128)S(1)} %bitcast.716, ...), kind=kLoop, calls=%fused_computation.242 | loop fusion | flops 6291456 | bytes 8388628 | tf_op jit(solution)/shard_map/add | solution.py:150
  671.8 9.5 %add_bitcast_fusion.12 = (f32[1,64,8,512]{3,0,2,1:T(1,128)S(1)}, f32[1,64,8,512]{3,0,2,1:T(1,128)S(1)}, f32[1,64,8,512]{3,0,2,1:T(1,128)S(1)}, f32[1,64,8,512]{3,0,2,1:T(1,128)S(1)}) fusion(f32[]{:T(128)S(6)} %sub.439, f32[]{:T(128)S(6)} %mul.3412, f32[]{:T(128)} %bitcast.40, f32[]{:T(128)} %bitcast.9, f32[2,64,2,8,512]{4,0,3,2,1:T(2,128)S(1)} %bitcast.717, ...), kind=kLoop, calls=%fused_computation.238 | loop fusion | flops 6291456 | bytes 8388628 | tf_op jit(solution)/shard_map/add | solution.py:150
  732.8 11.7 %all-to-all-start.4 = ((f32[2,1,8,128,512]{4,3,0,1,2:T(8,128)}), f32[2,1,8,128,512]{4,3,0,1,2:T(8,128)}, u32[]{:S(2)}, u32[]{:S(2)}) async-start(f32[2,1,8,128,512]{4,3,0,1,2:T(8,128)} %copy.768), calls=%async_computation.4 | async-start | bytes 8388608 | tf_op jit(solution)/shard_map/all_to_all | solution.py:229
  748.3 45.0 %all-to-all-done.4 = f32[2,1,8,128,512]{4,3,0,1,2:T(8,128)} async-done(((f32[2,1,8,128,512]{4,3,0,1,2:T(8,128)}), f32[2,1,8,128,512]{4,3,0,1,2:T(8,128)}, u32[]{:S(2)}, u32[]{:S(2)}) %all-to-all-start.4) | async-done | bytes 4194336 | tf_op jit(solution)/shard_map/all_to_all | solution.py:229
  800.0 4.4 fusion.50
  818.4 52.1 %all_to_all.39 = f32[2,8,1,128,512]{4,3,0,2,1:T(8,128)S(1)} all-to-all(f32[2,8,1,128,512]{4,3,0,2,1:T(8,128)S(1)} %copy.801), channel_id=1, replica_groups=mesh['spin'=8,'fock'=16] {'spin'}, dimensions={1} | all-to-all | bytes 8388608 | tf_op jit(solution)/shard_map/all_to_all | solution.py:236
  (465 shorter events, 384.8 us)
Async XLA Ops:
  4.2 10.0 %copy-start.10 = (f32[13]{0:T(128)S(1)}, f32[13]{0:T(128)}, u32[]{:S(2)}) copy-start(f32[13]{0:T(128)} %param.14) | copy-start | bytes 160
  4.2 10.7 %copy-start.11 = (f32[13]{0:T(128)S(1)}, f32[13]{0:T(128)}, u32[]{:S(2)}) copy-start(f32[13]{0:T(128)} %param.15) | copy-start | bytes 160
  4.2 12.1 %copy-start.8 = (f32[16]{0:T(128)S(1)}, f32[16]{0:T(128)}, u32[]{:S(2)}) copy-start(f32[16]{0:T(128)} %param.16) | copy-start | bytes 196
  4.2 12.1 %copy-start.9 = (s32[16]{0:T(128)S(1)}, s32[16]{0:T(128)}, u32[]{:S(2)}) copy-start(s32[16]{0:T(128)} %param.17) | copy-start | bytes 196
  5.8 36.6 %all-to-all-start = ((f32[16,2,32,512]{3,2,1,0:T(8,128)}), f32[16,2,32,512]{3,2,1,0:T(8,128)S(1)}, u32[]{:S(2)}, u32[]{:S(2)}) async-start(f32[16,2,32,512]{3,2,1,0:T(8,128)} %copy.690), calls=%async_computation | async-start | bytes 4194304 | tf_op jit(solution)/shard_map/all_to_all | solution.py:44
  42.4 29.9 %all-to-all-start.1 = ((f32[16,2,32,512]{3,2,1,0:T(8,128)}), f32[16,2,32,512]{3,2,1,0:T(8,128)}, u32[]{:S(2)}, u32[]{:S(2)}) async-start(f32[16,2,32,512]{3,2,1,0:T(8,128)} %copy.691), calls=%async_computation.1 | async-start | bytes 4194304 | tf_op jit(solution)/shard_map/all_to_all | solution.py:44
  75.6 8.2 copy-start.5
  90.5 3.5 copy-start.6
  103.4 8.6 copy-start.2
  112.0 3.7 copy-start.4
  120.7 3.5 copy-start.6
  133.6 8.6 copy-start.2
  142.2 3.7 copy-start.4
  150.9 3.5 copy-start.6
  163.9 8.6 copy-start.2
  172.5 3.7 copy-start.4
  181.1 3.5 copy-start.6
  194.1 8.6 copy-start.2
  202.7 3.7 copy-start.4
  211.3 3.5 copy-start.6
  224.3 8.6 copy-start.2
  232.9 3.7 copy-start.4
  254.5 8.6 copy-start.2
  263.1 3.7 copy-start.4
  284.7 8.6 copy-start.2
  293.3 3.7 copy-start.4
  314.9 8.6 copy-start.2
  323.5 3.7 copy-start.4
  345.1 8.6 copy-start.2
  353.7 3.7 copy-start.4
  375.4 8.6 copy-start.2
  384.0 3.7 copy-start.4
  405.6 8.6 copy-start.2
  414.2 3.7 copy-start.4
  422.8 3.5 copy-start.6
  435.8 8.6 copy-start.2
  444.4 3.7 copy-start.4
  466.0 8.6 copy-start.2
  474.6 3.7 copy-start.4
  483.3 3.5 copy-start.6
  496.2 8.6 copy-start.2
  504.8 3.7 copy-start.4
  526.4 8.6 copy-start.2
  535.0 3.7 copy-start.4
  552.2 35.1 %copy-start.12 = (s32[13]{0:T(128)S(1)}, s32[13]{0:T(128)}, u32[]{:S(2)}) copy-start(s32[13]{0:T(128)} %param.18) | copy-start | bytes 160
  552.2 48.3 %copy-start.13 = (f32[13]{0:T(128)S(1)}, f32[13]{0:T(128)}, u32[]{:S(2)}) copy-start(f32[13]{0:T(128)} %param.19) | copy-start | bytes 160
  582.8 27.7 %all-to-all-start.3 = ((f32[16,2,32,512]{3,1,2,0:T(2,128)}), f32[16,2,32,512]{3,1,2,0:T(2,128)}, u32[]{:S(2)}, u32[]{:S(2)}) async-start(f32[16,2,32,512]{3,1,2,0:T(2,128)} %get-tuple-element.460), calls=%async_computation.3 | async-start | bytes 4194304 | tf_op jit(solution)/shard_map/all_to_all | solution.py:44
  732.8 60.5 %all-to-all-start.4 = ((f32[2,1,8,128,512]{4,3,0,1,2:T(8,128)}), f32[2,1,8,128,512]{4,3,0,1,2:T(8,128)}, u32[]{:S(2)}, u32[]{:S(2)}) async-start(f32[2,1,8,128,512]{4,3,0,1,2:T(8,128)} %copy.768), calls=%async_computation.4 | async-start | bytes 8388608 | tf_op jit(solution)/shard_map/all_to_all | solution.py:229
  (42 other events, 120.8 us)
where the time goes:
time: 883 us; the launch traced here: 874 us
  other arithmetic  390 us (44%)
  local copies, waits for them, and re-layouts  256 us (29%)
  waiting for transfers between devices  95.7 us (11%)
  blocking collectives  82.7 us (9%)
  starting transfers between devices  29 us (3%)
  between operations  18.7 us (2%)
    add x15, other arithmetic, advance(): total + weighted_term(following, real_weights[term_index], imag_weights[t...  129 us
    while x180, local copies, waits for them, and re-layouts  110 us
    sub x15, other arithmetic, advance(): following = 2.0 * apply_operator(present) - previous  82.2 us
    slice x16, local copies, waits for them, and re-layouts, apply_hamiltonian(): previous_sub = jnp.pad(center[:, :, :-1], ((0, 0), (0, 0), (1, 0)))  53 us
    all_to_all x1, blocking collectives, per_device(): lax.all_to_all(moved.reshape(2, spin_count, 1, rest, column_count), 'spin...  52.1 us
    all_to_all x3, waiting for transfers between devices, several_exchanges(): lax.all_to_all(slab, axis, split_axis=0, concat_axis=0, tiled=True)  50.7 us
    all_to_all x1, waiting for transfers between devices, per_device(): lax.all_to_all(grouped, 'spin', split_axis=2, concat_axis=1, tiled=True)  45 us
    add x10, other arithmetic, partner_term(): cosine * own_part[0]  40.8 us
  transfers between devices with their start and end apart: 4, of which 4 were waited for; matrix products, arithmetic and copies ran while one was open for 1% of the time, Pallas kernels for 0%

commit v1 on v0

v1 whole, which is shorter than its diff:
```python
import math

import jax
import jax.numpy as jnp
from jax import lax
from jax.experimental import pallas as pl
from jax.experimental.pallas import tpu as pltpu
from jax.sharding import PartitionSpec as P

SPINS = 13
FA = 512
FB = 16
FROZEN = 16
DEGREE = 16
MESH_ID = pl.DeviceIdType.MESH

evolve_time = 12.0
diagonal_first = 0.06
diagonal_second = 0.04
ladder_first = 0.35
ladder_second = 0.1

PLACES = 8
CHUNKS = 8
GROUP = 16
LANES = PLACES * GROUP
OWN = 32
HALO = DEGREE
LEVELS = OWN + 2 * HALO
PADDED = LEVELS + 4
COLS = OWN * FB
SIDE = HALO * FB
LANE_BITS = (0, 1, 2, 3, 10, 11, 12)
AHEAD = 2


def bessel_first(term_order, argument):
    running = 0.0
    addend = (argument / 2.0) ** term_order / math.factorial(term_order)
    for serial in range(80):
        running = running + addend
        addend = addend * -(argument * argument / 4.0) / ((serial + 1) * (serial + 1 + term_order))
    return running


OMEGA = [(1.0 if k == 0 else 2.0) * bessel_first(k, evolve_time) for k in range(DEGREE + 1)]


def iota(shape, dim):
    return lax.broadcasted_iota(jnp.int32, shape, dim)


def fill_rotations(angles, drive_bits, rot):
    for j in range(SPINS):
        angle = jnp.full((8, 128), angles[j], jnp.float32)
        phase = jnp.full((8, 128), drive_bits[j], jnp.int32).astype(jnp.float32)
        sine = jnp.sin(angle)
        rot[3 * j] = jnp.cos(angle)
        rot[3 * j + 1] = sine * phase
        rot[3 * j + 2] = sine * (1.0 - phase)


def fill_mixer(rot, mix_hi, mix_lo):
    def rows(step, carry):
        base = pl.multiple_of(step * 16, 16)
        out_lane = base + iota((16, 128), 0)
        in_lane = iota((16, 128), 1)
        real = jnp.ones((16, 128), jnp.float32)
        imag = jnp.zeros((16, 128), jnp.float32)
        for place, bit in enumerate(LANE_BITS):
            out_bit = (out_lane >> place) & 1
            in_bit = (in_lane >> place) & 1
            same = out_bit == in_bit
            cosine = jnp.concatenate([rot[3 * bit]] * 2, axis=0)
            driven = jnp.concatenate([rot[3 * bit + 1]] * 2, axis=0)
            kept = jnp.concatenate([rot[3 * bit + 2]] * 2, axis=0)
            f_real = jnp.where(same, cosine, jnp.where(out_bit == 1, driven, -driven))
            f_imag = jnp.where(same, 0.0, -kept)
            real, imag = real * f_real - imag * f_imag, real * f_imag + imag * f_real
        top = jnp.concatenate([real, -imag], axis=1)
        low = jnp.concatenate([imag, real], axis=1)
        for start, value in ((0, top), (128, low)):
            high = value.astype(jnp.bfloat16)
            rest = (value - high.astype(jnp.float32)).astype(jnp.bfloat16)
            mix_hi[pl.ds(start + base, 16), :] = high
            mix_lo[pl.ds(start + base, 16), :] = rest
        return carry

    lax.fori_loop(0, 8, rows, 0)


def fill_diagonal(fock_place, diag):
    def rows(n, carry):
        row = iota((16, 128), 0)
        m = 2 * (row % 8) + row // 8
        level = fock_place * OWN - HALO + n
        level_float = jnp.full((16, 128), level, jnp.int32).astype(jnp.float32)
        value = diagonal_first * (2.0 * level_float / (FA - 1) - 1.0) + diagonal_second * (
            2.0 * m.astype(jnp.float32) / (FB - 1) - 1.0
        )
        diag[pl.ds(pl.multiple_of(n * 16, 16), 16), :] = 2.0 * value
        return carry

    lax.fori_loop(0, PADDED, rows, 0)


def strengths(chunk, spin_place, coupling_first, coupling_second, frozen_coupling, frozen_bits):
    shape = (8, 128)
    lane = iota(shape, 1)
    config = (lane >> 4) * 1024 + (spin_place * CHUNKS + chunk) * GROUP + (lane & 15)
    first = jnp.zeros(shape, jnp.float32)
    second = jnp.zeros(shape, jnp.float32)
    total_first = jnp.zeros(shape, jnp.float32)
    total_second = jnp.zeros(shape, jnp.float32)
    for j in range(SPINS):
        sign = (1 - 2 * ((config >> j) & 1)).astype(jnp.float32)
        first = first + coupling_first[j] * sign
        second = second + coupling_second[j] * sign
        total_first = total_first + coupling_first[j]
        total_second = total_second + coupling_second[j]
    for k in range(FROZEN):
        sign = jnp.full(shape, 1 - 2 * frozen_bits[k], jnp.int32).astype(jnp.float32)
        first = first + frozen_coupling[k] * sign
        total_first = total_first + frozen_coupling[k]
    return ladder_first * first / total_first, ladder_second * second / total_second


def butterfly(real, imag, rot, bits):
    count = len(real)
    for place, bit in enumerate(bits):
        cosine, driven, kept = rot[3 * bit], rot[3 * bit + 1], rot[3 * bit + 2]
        step = 1 << place
        for low in range(count):
            if low & step:
                continue
            up = low | step
            lr, li, ur, ui = real[low], imag[low], real[up], imag[up]
            real[low] = cosine * lr - driven * ur + kept * ui
            imag[low] = cosine * li - driven * ui - kept * ur
            real[up] = cosine * ur + driven * lr + kept * li
            imag[up] = cosine * ui + driven * li - kept * lr
    return real, imag


def kernel(
    x,
    cutoffs,
    coupling_first,
    coupling_second,
    frozen_coupling,
    frozen_bits,
    drive_bits,
    angles,
    out,
    inb,
    cut_all,
    left,
    right,
    nat_re,
    nat_im,
    vec_re,
    vec_im,
    even_re,
    even_im,
    odd_re,
    odd_im,
    y_re,
    y_im,
    diag,
    ladder,
    rot,
    mix_hi,
    mix_lo,
    outb,
    back,
    in_send,
    in_recv,
    cut_send,
    cut_recv,
    halo_send,
    halo_recv,
    out_send,
    out_recv,
    store_sem,
):
    s = lax.axis_index("spin")
    f = lax.axis_index("fock")
    f_left = (f + 15) % 16
    f_right = (f + 1) % 16

    barrier = pltpu.get_barrier_semaphore()
    for k in range(1, PLACES):
        pl.semaphore_signal(barrier, inc=1, device_id=((s + k) % PLACES, f), device_id_type=MESH_ID)
    for near in (f_left, f_right):
        pl.semaphore_signal(barrier, inc=1, device_id=(s, near), device_id_type=MESH_ID)
    pl.semaphore_wait(barrier, PLACES + 1)

    def cut_copy(k):
        p = (s + k) % PLACES
        if k == 0:
            return pltpu.make_async_copy(cutoffs.at[s], cut_all.at[s], cut_recv.at[0])
        return pltpu.make_async_remote_copy(
            src_ref=cutoffs.at[p],
            dst_ref=cut_all.at[s],
            send_sem=cut_send.at[k],
            recv_sem=cut_recv.at[k],
            device_id=(p, f),
            device_id_type=MESH_ID,
        )

    def in_copy(i, k):
        p = (s + k) % PLACES
        src = x.at[:, pl.ds(pl.multiple_of((p * CHUNKS + i) * GROUP, GROUP), GROUP), :]
        dst = inb.at[i, :, pl.ds(pl.multiple_of(s * GROUP, GROUP), GROUP), :]
        if k == 0:
            return pltpu.make_async_copy(src, dst, in_recv.at[i, 0])
        return pltpu.make_async_remote_copy(
            src_ref=src,
            dst_ref=dst,
            send_sem=in_send.at[i, k],
            recv_sem=in_recv.at[i, k],
            device_id=(p, f),
            device_id_type=MESH_ID,
        )

    def halo_copy(i, side):
        if side == 0:
            src, dst, near = inb.at[i, :, :, pl.ds(COLS - SIDE, SIDE)], left.at[i], f_right
        else:
            src, dst, near = inb.at[i, :, :, pl.ds(0, SIDE)], right.at[i], f_left
        return pltpu.make_async_remote_copy(
            src_ref=src,
            dst_ref=dst,
            send_sem=halo_send.at[i, side],
            recv_sem=halo_recv.at[i, side],
            device_id=(s, near),
            device_id_type=MESH_ID,
        )

    def out_copy(i, k):
        p = (s + k) % PLACES
        src = outb.at[i, :, pl.ds(pl.multiple_of(p * GROUP, GROUP), GROUP), :]
        dst = back.at[:, pl.ds(pl.multiple_of((s * CHUNKS + i) * GROUP, GROUP), GROUP), :]
        if k == 0:
            return pltpu.make_async_copy(src, dst, out_recv.at[i, 0])
        return pltpu.make_async_remote_copy(
            src_ref=src,
            dst_ref=dst,
            send_sem=out_send.at[i, k],
            recv_sem=out_recv.at[i, k],
            device_id=(p, f),
            device_id_type=MESH_ID,
        )

    def wait_arrival(copy, k):
        if k == 0:
            copy.wait()
        else:
            copy.wait_recv()

    order = (4, 3, 5, 2, 6, 1, 7, 0)
    for k in order:
        cut_copy(k).start()

    def start_in(i, carry):
        for k in order:
            in_copy(i, k).start()
        return carry

    lax.fori_loop(0, CHUNKS, start_in, 0)

    fill_rotations(angles, drive_bits, rot)
    fill_mixer(rot, mix_hi, mix_lo)
    fill_diagonal(f, diag)
    for k in range(PLACES):
        wait_arrival(cut_copy(k), k)

    def forward(i):
        for k in range(PLACES):
            wait_arrival(in_copy(i, k), k)
        halo_copy(i, 0).start()
        halo_copy(i, 1).start()

    for i in range(AHEAD):
        forward(i)

    def series_step(k, i, coef):
        link, low_side, high_side = coef
        source_re, source_im = (odd_re, odd_im) if k % 2 == 0 else (even_re, even_im)
        target_re, target_im = (even_re, even_im) if k % 2 == 0 else (odd_re, odd_im)
        start = HALO - k
        groups = -(-(OWN + 2 * k) // 4)

        def group(g, carry):
            n0 = start + 4 * g

            def tile(ref, j, t):
                return ref[pl.ds(pl.multiple_of((n0 + j) * 16 + t * 8, 8), 8), :]

            steps = [ladder[pl.ds(n0 + j, 8, stride=0), :] for j in range(5)]
            diagonal = [[tile(diag, j, t) for t in range(2)] for j in range(4)]
            for source, target, vec, sign, y in (
                (source_im, target_re, vec_re, 1, y_re),
                (source_re, target_im, vec_im, -1, y_im),
            ):
                p = [[tile(source, j, t) for t in range(2)] for j in range(-1, 5)]
                for j in range(4):
                    for t in range(2):
                        own = p[j + 1][t]
                        other = p[j + 1][1 - t]
                        far = pltpu.roll(other, 1 if t == 0 else 7, axis=0)
                        applied = (
                            diagonal[j][t] * own
                            + link * other
                            + (low_side if t == 0 else high_side) * far
                            + (steps[j] * p[j][t] + steps[j + 1] * p[j + 2][t])
                        )
                        if k == 0:
                            applied = 0.5 * applied
                        kept = OMEGA[k] * tile(vec, j, t)
                        if k < DEGREE - 1:
                            kept = kept + tile(target, j, t)
                        value = kept + applied if sign > 0 else kept - applied
                        if k == 0:
                            row = (n0 + j - HALO) * 16 + t
                            y[pl.ds(row, 8, stride=2), :] = value
                        else:
                            target[pl.ds(pl.multiple_of((n0 + j) * 16 + t * 8, 8), 8), :] = value
            return carry

        lax.fori_loop(0, groups, group, 0)

    def chunk(i, carry):
        @pl.when(i < CHUNKS - AHEAD)
        def _():
            forward(i + AHEAD)

        strength_first, strength_second = strengths(
            i, s, coupling_first, coupling_second, frozen_coupling, frozen_bits
        )
        cut = jnp.zeros((8, 128), jnp.int32)
        lane_place = iota((8, 128), 1) >> 4
        for q in range(PLACES):
            row = jnp.broadcast_to(cut_all[q], (8, 128))
            turned = pltpu.roll(row, ((q + 8 - i) * GROUP) % 128, axis=1)
            cut = jnp.where(lane_place == q, turned, cut)
        for block in range(9):
            level = f * OWN - HALO + block * 8 + iota((8, 128), 0)
            root = jnp.sqrt(jnp.maximum(level, 0).astype(jnp.float32) / FA)
            ladder[pl.ds(block * 8, 8), :] = jnp.where(
                (level >= 1) & (level < cut), 2.0 * strength_first * root, 0.0
            )
        sub = iota((8, 128), 0).astype(jnp.float32)
        double = 2.0 * strength_second
        link = double * jnp.sqrt((2.0 * sub + 1.0) / FB)
        low_side = double * jnp.sqrt(2.0 * sub / FB)
        high_side = jnp.where(sub < 7.0, double * jnp.sqrt((2.0 * sub + 2.0) / FB), 0.0)

        halo_copy(i, 0).wait_recv()
        halo_copy(i, 1).wait_recv()

        for part, natural in ((0, nat_re), (1, nat_im)):
            for b in range(8):
                if b < 2:
                    piece = left[i, part, :, b * 128 : (b + 1) * 128]
                elif b < 6:
                    piece = inb[i, part, :, (b - 2) * 128 : (b - 1) * 128]
                else:
                    piece = right[i, part, :, (b - 6) * 128 : (b - 5) * 128]
                natural[b * 128 : (b + 1) * 128, :] = piece.T

        def first_term(n, c):
            for natural, vec, even in ((nat_re, vec_re, even_re), (nat_im, vec_im, even_im)):
                for j in range(4):
                    for t in range(2):
                        value = natural[pl.ds((n * 4 + j) * 16 + t, 8, stride=2), :]
                        place = pl.ds(pl.multiple_of((n * 4 + j) * 16 + t * 8, 8), 8)
                        vec[place, :] = value
                        even[place, :] = OMEGA[DEGREE] * value
            return c

        lax.fori_loop(0, LEVELS // 4, first_term, 0)
        for k in range(DEGREE - 1, -1, -1):
            series_step(k, i, (link, low_side, high_side))

        y = jnp.concatenate([y_re[...], y_im[...]], axis=1)
        y_hi = y.astype(jnp.bfloat16)
        y_lo = (y - y_hi.astype(jnp.float32)).astype(jnp.bfloat16)

        def product(a, b):
            return lax.dot_general(
                a, b, (((1,), (1,)), ((), ())), preferred_element_type=jnp.float32
            )

        mixed = (
            product(mix_hi[...], y_hi) + product(mix_hi[...], y_lo) + product(mix_lo[...], y_hi)
        )
        outb[i, 0] = mixed[:LANES]
        outb[i, 1] = mixed[LANES:]
        for k in order:
            out_copy(i, k).start()
        return carry

    lax.fori_loop(0, CHUNKS, chunk, 0)

    def rotate_places(i, carry):
        for k in range(PLACES):
            wait_arrival(out_copy(i, k), k)

        def unit(u, c):
            half, col = u // 4, u % 4

            def spot(q):
                row = pl.multiple_of((q * CHUNKS + i) * GROUP + half * 8, 8)
                return pl.ds(row, 8), pl.ds(pl.multiple_of(col * 128, 128), 128)

            real = [back[0, spot(q)[0], spot(q)[1]] for q in range(PLACES)]
            imag = [back[1, spot(q)[0], spot(q)[1]] for q in range(PLACES)]
            real, imag = butterfly(real, imag, rot, (7, 8, 9))
            for q in range(PLACES):
                back[0, spot(q)[0], spot(q)[1]] = real[q]
                back[1, spot(q)[0], spot(q)[1]] = imag[q]
            return c

        lax.fori_loop(0, 8, unit, 0)
        return carry

    lax.fori_loop(0, CHUNKS, rotate_places, 0)

    def store_copy(q):
        rows = pl.ds(pl.multiple_of(q * 128, 128), 128)
        return pltpu.make_async_copy(back.at[:, rows, :], out.at[:, rows, :], store_sem.at[q])

    def rotate_chunks(q, carry):
        def unit(u, c):
            half, col = u // 4, u % 4

            def spot(i):
                row = pl.multiple_of((q * CHUNKS + i) * GROUP + half * 8, 8)
                return pl.ds(row, 8), pl.ds(pl.multiple_of(col * 128, 128), 128)

            real = [back[0, spot(i)[0], spot(i)[1]] for i in range(CHUNKS)]
            imag = [back[1, spot(i)[0], spot(i)[1]] for i in range(CHUNKS)]
            real, imag = butterfly(real, imag, rot, (4, 5, 6))
            for i in range(CHUNKS):
                back[0, spot(i)[0], spot(i)[1]] = real[i]
                back[1, spot(i)[0], spot(i)[1]] = imag[i]
            return c

        lax.fori_loop(0, 8, unit, 0)
        store_copy(q).start()
        return carry

    lax.fori_loop(0, PLACES, rotate_chunks, 0)

    def finish(i, carry):
        for k in range(1, PLACES):
            in_copy(i, k).wait_send()
            out_copy(i, k).wait_send()
        halo_copy(i, 0).wait_send()
        halo_copy(i, 1).wait_send()
        store_copy(i).wait()
        return carry

    lax.fori_loop(0, CHUNKS, finish, 0)
    for k in range(1, PLACES):
        cut_copy(k).wait_send()


def per_device(
    amplitudes,
    cutoffs,
    coupling_first,
    coupling_second,
    frozen_coupling,
    frozen_bits,
    drive_bits,
    angles,
):
    f32 = jnp.float32
    padded = pltpu.VMEM((PADDED * FB, LANES), f32)
    dma = pltpu.SemaphoreType.DMA
    smem = pl.BlockSpec(memory_space=pltpu.SMEM)
    return pl.pallas_call(
        kernel,
        name="evolve_and_rotate",
        out_shape=jax.ShapeDtypeStruct(amplitudes.shape, f32),
        in_specs=[
            pl.BlockSpec(memory_space=pl.ANY),
            pl.BlockSpec(memory_space=pltpu.VMEM),
            smem,
            smem,
            smem,
            smem,
            smem,
            smem,
        ],
        out_specs=pl.BlockSpec(memory_space=pl.ANY),
        scratch_shapes=[
            pltpu.VMEM((CHUNKS, 2, LANES, COLS), f32),
            pltpu.VMEM((PLACES, 1, 128), jnp.int32),
            pltpu.VMEM((CHUNKS, 2, LANES, SIDE), f32),
            pltpu.VMEM((CHUNKS, 2, LANES, SIDE), f32),
            pltpu.VMEM((LEVELS * FB, LANES), f32),
            pltpu.VMEM((LEVELS * FB, LANES), f32),
            padded,
            padded,
            padded,
            padded,
            padded,
            padded,
            pltpu.VMEM((COLS, LANES), f32),
            pltpu.VMEM((COLS, LANES), f32),
            padded,
            pltpu.VMEM((72, LANES), f32),
            pltpu.VMEM((3 * SPINS, 8, 128), f32),
            pltpu.VMEM((2 * LANES, 2 * LANES), jnp.bfloat16),
            pltpu.VMEM((2 * LANES, 2 * LANES), jnp.bfloat16),
            pltpu.VMEM((CHUNKS, 2, LANES, COLS), f32),
            pltpu.VMEM((2, CHUNKS * LANES, COLS), f32),
            dma((CHUNKS, PLACES)),
            dma((CHUNKS, PLACES)),
            dma((PLACES,)),
            dma((PLACES,)),
            dma((CHUNKS, 2)),
            dma((CHUNKS, 2)),
            dma((CHUNKS, PLACES)),
            dma((CHUNKS, PLACES)),
            dma((PLACES,)),
        ],
        compiler_params=pltpu.CompilerParams(
            collective_id=0, has_side_effects=True, vmem_limit_bytes=60 << 20
        ),
    )(
        amplitudes,
        cutoffs.reshape(PLACES, 1, 128),
        coupling_first,
        coupling_second,
        frozen_coupling,
        frozen_bits,
        drive_bits,
        angles,
    )


def solution(mesh):
    placed = (P(None, "spin", "fock"), P("spin"), P(), P(), P(), P(), P(), P())
    return jax.shard_map(
        per_device, mesh=mesh, in_specs=placed, out_specs=P(None, "spin", "fock"), check_vma=False
    )
```

time: 883 us -> 113 us (0.13); the launches traced: 874 us -> 113 us
  other arithmetic: 390 us -> 0 us
  local copies, waits for them, and re-layouts: 256 us -> 4.64 us
  Pallas kernels: 0 us -> 108 us
  waiting for transfers between devices: 95.7 us -> 0 us
  blocking collectives: 82.7 us -> 0 us
  starting transfers between devices: 29 us -> 0 us
  between operations: 18.7 us -> 0.01 us
    add x56 -> x0, other arithmetic: 209 us -> none  [the longest x15 129 us: advance(): total + weighted_term(following, real_weights[term_index], imag_weights[t...]
    while x180 -> x0, local copies, waits for them, and re-layouts: 110 us -> none
    pallas_call x0 -> x1, Pallas kernels: none -> 108 us  [per_device(): pl.pallas_call(kernel, name='evolve_and_rotate', out_shape=jax.ShapeDtype...]
    all_to_all x4 -> x0, waiting for transfers between devices: 95.7 us -> none  [the longest x3 50.7 us: several_exchanges(): lax.all_to_all(slab, axis, split_axis=0, concat_axis=0, tiled=True)]
    all_to_all x2 -> x0, blocking collectives: 82.7 us -> none  [the longest x1 52.1 us: per_device(): lax.all_to_all(moved.reshape(2, spin_count, 1, rest, column_count), 'spin...]
    sub x15 -> x0, other arithmetic: 82.2 us -> none  [advance(): following = 2.0 * apply_operator(present) - previous]
    slice x21 -> x0, local copies, waits for them, and re-layouts: 67 us -> none  [the longest x16 53 us: apply_hamiltonian(): previous_sub = jnp.pad(center[:, :, :-1], ((0, 0), (0, 0), (1, 0)))]
    select_n x48 -> x0, other arithmetic: 34.1 us -> none  [the longest x16 33.6 us: apply_hamiltonian(): jnp.where((level_index >= 1) & (level_index < cutoff), jnp.sqrt(jnp.maxim...]
  transfers between devices with their start and end apart: 4 -> 0, of which waited for: 4 -> 0; matrix products, arithmetic and copies ran while one was open for 1% -> 0% of each run, Pallas kernels for 0% -> 0%
where the time goes in v1:
time: 113 us
  Pallas kernels  108 us (96%)
  local copies, waits for them, and re-layouts  4.64 us (4%)
    pallas_call x1, Pallas kernels, per_device(): pl.pallas_call(kernel, name='evolve_and_rotate', out_shape=jax.ShapeDtype...  108 us
    unnamed x1, local copies, waits for them, and re-layouts  4.64 us

profile of v1, /device:TPU:1, one launch (start us, length us, event | category | flops | bytes accessed | tf_op | source)
XLA Modules:
  0.0 112.8 jit_solution(15927856906004880387)
XLA Ops:
  0.0 108.2 %evolve_and_rotate.1 = f32[2,1024,512]{2,1,0:T(8,128)} custom-call(f32[2,1024,512]{2,1,0:T(8,128)} %x.1, s32[8,1,128]{2,1,0:T(1,128)} %bitcast.1, f32[13]{0:T(128)} %coupling_first.1, f32[13]{0:T(128)} %coupling_second.1, f32[16]{0:T(128)} %frozen_coupling.1, s32[16]{0:T(128)} %frozen_bits.1, s32[13]{0:T(128)} %drive_bits.1, f32[13]{0:T(128)} %angles.1), custom_call_target="tpu_custom_call" | custom-call | tf_op jit(solution)/shard_map/evolve_and_rotate/pallas_call | solution.py:484
  108.2 4.6 %copy.10 = f32[2,1024,512]{2,1,0:T(8,128)} copy(f32[2,1024,512]{2,1,0:T(8,128)} %evolve_and_rotate.1) | data formatting | bytes 8388608

commit v2 on v1

--- a/solution.py
+++ b/solution.py
@@ -125,10 +125,9 @@
     return ladder_first * first / total_first, ladder_second * second / total_second
 
 
-def butterfly(real, imag, rot, bits):
+def butterfly(real, imag, bits):
     count = len(real)
-    for place, bit in enumerate(bits):
-        cosine, driven, kept = rot[3 * bit], rot[3 * bit + 1], rot[3 * bit + 2]
+    for place, (cosine, driven, kept) in bits:
         step = 1 << place
         for low in range(count):
             if low & step:
@@ -151,7 +150,8 @@
     frozen_bits,
     drive_bits,
     angles,
-    out,
+    back,
+    rot_out,
     inb,
     cut_all,
     left,
@@ -172,7 +172,6 @@
     mix_hi,
     mix_lo,
     outb,
-    back,
     in_send,
     in_recv,
     cut_send,
@@ -181,7 +180,6 @@
     halo_recv,
     out_send,
     out_recv,
-    store_sem,
 ):
     s = lax.axis_index("spin")
     f = lax.axis_index("fock")
@@ -331,10 +329,6 @@
         lax.fori_loop(0, groups, group, 0)
 
     def chunk(i, carry):
-        @pl.when(i < CHUNKS - AHEAD)
-        def _():
-            forward(i + AHEAD)
-
         strength_first, strength_second = strengths(
             i, s, coupling_first, coupling_second, frozen_coupling, frozen_bits
         )
@@ -399,11 +393,19 @@
         outb[i, 1] = mixed[LANES:]
         for k in order:
             out_copy(i, k).start()
+
+        @pl.when(i < CHUNKS - AHEAD)
+        def _():
+            forward(i + AHEAD)
+
         return carry
 
     lax.fori_loop(0, CHUNKS, chunk, 0)
 
-    def rotate_places(i, carry):
+    def turn(bit):
+        return rot[3 * bit], rot[3 * bit + 1], rot[3 * bit + 2]
+
+    def rotate_places(i):
         for k in range(PLACES):
             wait_arrival(out_copy(i, k), k)
 
@@ -416,42 +418,41 @@
 
             real = [back[0, spot(q)[0], spot(q)[1]] for q in range(PLACES)]
             imag = [back[1, spot(q)[0], spot(q)[1]] for q in range(PLACES)]
-            real, imag = butterfly(real, imag, rot, (7, 8, 9))
+            turns = [(place, turn(7 + place)) for place in range(3)]
+            real, imag = butterfly(real, imag, turns)
             for q in range(PLACES):
                 back[0, spot(q)[0], spot(q)[1]] = real[q]
                 back[1, spot(q)[0], spot(q)[1]] = imag[q]
             return c
 
         lax.fori_loop(0, 8, unit, 0)
-        return carry
-
-    lax.fori_loop(0, CHUNKS, rotate_places, 0)
-
-    def store_copy(q):
-        rows = pl.ds(pl.multiple_of(q * 128, 128), 128)
-        return pltpu.make_async_copy(back.at[:, rows, :], out.at[:, rows, :], store_sem.at[q])
-
-    def rotate_chunks(q, carry):
+
+    def rotate_pair(pair, carry):
+        rotate_places(2 * pair)
+        rotate_places(2 * pair + 1)
+
         def unit(u, c):
-            half, col = u // 4, u % 4
-
-            def spot(i):
-                row = pl.multiple_of((q * CHUNKS + i) * GROUP + half * 8, 8)
-                return pl.ds(row, 8), pl.ds(pl.multiple_of(col * 128, 128), 128)
-
-            real = [back[0, spot(i)[0], spot(i)[1]] for i in range(CHUNKS)]
-            imag = [back[1, spot(i)[0], spot(i)[1]] for i in range(CHUNKS)]
-            real, imag = butterfly(real, imag, rot, (4, 5, 6))
-            for i in range(CHUNKS):
-                back[0, spot(i)[0], spot(i)[1]] = real[i]
-                back[1, spot(i)[0], spot(i)[1]] = imag[i]
+            q, col = u // 4, u % 4
+            base = (q * CHUNKS + 2 * pair) * GROUP
+            cols = pl.ds(pl.multiple_of(col * 128, 128), 128)
+            for half in range(2):
+                rows = [
+                    pl.ds(pl.multiple_of(base + e * GROUP + half * 8, 8), 8) for e in range(2)
+                ]
+                real = [back[0, r, cols] for r in rows]
+                imag = [back[1, r, cols] for r in rows]
+                real, imag = butterfly(real, imag, [(0, turn(4))])
+                for e in range(2):
+                    back[0, rows[e], cols] = real[e]
+                    back[1, rows[e], cols] = imag[e]
             return c
 
-        lax.fori_loop(0, 8, unit, 0)
-        store_copy(q).start()
-        return carry
-
-    lax.fori_loop(0, PLACES, rotate_chunks, 0)
+        lax.fori_loop(0, 4 * PLACES, unit, 0)
+        return carry
+
+    for j in range(6):
+        rot_out[j] = rot[15 + j]
+    lax.fori_loop(0, CHUNKS // 2, rotate_pair, 0)
 
     def finish(i, carry):
         for k in range(1, PLACES):
@@ -459,12 +460,46 @@
             out_copy(i, k).wait_send()
         halo_copy(i, 0).wait_send()
         halo_copy(i, 1).wait_send()
-        store_copy(i).wait()
         return carry
 
     lax.fori_loop(0, CHUNKS, finish, 0)
     for k in range(1, PLACES):
         cut_copy(k).wait_send()
+
+
+def last_kernel(back, rot, out, done, sems):
+    def store_copy(q):
+        rows = pl.ds(pl.multiple_of(q * 128, 128), 128)
+        return pltpu.make_async_copy(done.at[:, rows, :], out.at[:, rows, :], sems.at[q])
+
+    def rotate_chunks(q, carry):
+        def unit(u, c):
+            half, col = u // 4, u % 4
+
+            def spot(i):
+                row = pl.multiple_of((q * CHUNKS + i) * GROUP + half * 8, 8)
+                return pl.ds(row, 8), pl.ds(pl.multiple_of(col * 128, 128), 128)
+
+            real = [back[0, spot(i)[0], spot(i)[1]] for i in range(CHUNKS)]
+            imag = [back[1, spot(i)[0], spot(i)[1]] for i in range(CHUNKS)]
+            turns = [(1, (rot[0], rot[1], rot[2])), (2, (rot[3], rot[4], rot[5]))]
+            real, imag = butterfly(real, imag, turns)
+            for i in range(CHUNKS):
+                done[0, spot(i)[0], spot(i)[1]] = real[i]
+                done[1, spot(i)[0], spot(i)[1]] = imag[i]
+            return c
+
+        lax.fori_loop(0, 8, unit, 0)
+        store_copy(q).start()
+        return carry
+
+    lax.fori_loop(0, PLACES, rotate_chunks, 0)
+
+    def finish(q, carry):
+        store_copy(q).wait()
+        return carry
+
+    lax.fori_loop(0, PLACES, finish, 0)
 
 
 def per_device(
@@ -481,10 +516,14 @@
     padded = pltpu.VMEM((PADDED * FB, LANES), f32)
     dma = pltpu.SemaphoreType.DMA
     smem = pl.BlockSpec(memory_space=pltpu.SMEM)
-    return pl.pallas_call(
+    vmem = pl.BlockSpec(memory_space=pltpu.VMEM)
+    back, rot = pl.pallas_call(
         kernel,
         name="evolve_and_rotate",
-        out_shape=jax.ShapeDtypeStruct(amplitudes.shape, f32),
+        out_shape=[
+            pltpu.VMEM((2, CHUNKS * LANES, COLS), f32),
+            pltpu.VMEM((6, 8, 128), f32),
+        ],
         in_specs=[
             pl.BlockSpec(memory_space=pl.ANY),
             pl.BlockSpec(memory_space=pltpu.VMEM),
@@ -495,7 +534,7 @@
             smem,
             smem,
         ],
-        out_specs=pl.BlockSpec(memory_space=pl.ANY),
+        out_specs=[vmem, vmem],
         scratch_shapes=[
             pltpu.VMEM((CHUNKS, 2, LANES, COLS), f32),
             pltpu.VMEM((PLACES, 1, 128), jnp.int32),
@@ -517,7 +556,6 @@
             pltpu.VMEM((2 * LANES, 2 * LANES), jnp.bfloat16),
             pltpu.VMEM((2 * LANES, 2 * LANES), jnp.bfloat16),
             pltpu.VMEM((CHUNKS, 2, LANES, COLS), f32),
-            pltpu.VMEM((2, CHUNKS * LANES, COLS), f32),
             dma((CHUNKS, PLACES)),
             dma((CHUNKS, PLACES)),
             dma((PLACES,)),
@@ -526,10 +564,9 @@
             dma((CHUNKS, 2)),
             dma((CHUNKS, PLACES)),
             dma((CHUNKS, PLACES)),
-            dma((PLACES,)),
         ],
         compiler_params=pltpu.CompilerParams(
-            collective_id=0, has_side_effects=True, vmem_limit_bytes=60 << 20
+            collective_id=0, has_side_effects=True, vmem_limit_bytes=62_800_000
         ),
     )(
         amplitudes,
@@ -541,6 +578,15 @@
         drive_bits,
         angles,
     )
+    return pl.pallas_call(
+        last_kernel,
+        name="rotate_last",
+        out_shape=jax.ShapeDtypeStruct(amplitudes.shape, f32),
+        in_specs=[vmem, vmem],
+        out_specs=pl.BlockSpec(memory_space=pl.ANY),
+        scratch_shapes=[pltpu.VMEM(amplitudes.shape, f32), dma((PLACES,))],
+        compiler_params=pltpu.CompilerParams(vmem_limit_bytes=16 << 20),
+    )(back, rot)
 
 
 def solution(mesh):

time: 113 us -> 109 us (0.965)
  local copies, waits for them, and re-layouts: 4.64 us -> 0 us
    unnamed x1 -> x0, local copies, waits for them, and re-layouts: 4.64 us -> none
    pallas_call x1 -> x2, Pallas kernels: 108 us -> 108 us  [the longest x1 105 us: per_device(): pl.pallas_call(kernel, name='evolve_and_rotate', out_shape=[pltpu.VMEM((2...]
where the time goes in v2:
time: 109 us; the launch traced here: 108 us
  Pallas kernels  108 us (99%)
    pallas_call x1, Pallas kernels, per_device(): pl.pallas_call(kernel, name='evolve_and_rotate', out_shape=[pltpu.VMEM((2...  105 us
    pallas_call x1, Pallas kernels, per_device(): pl.pallas_call(last_kernel, name='rotate_last', out_shape=jax.ShapeDtypeS...  3.26 us

profile of v2, /device:TPU:1, one launch (start us, length us, event | category | flops | bytes accessed | tf_op | source)
XLA Modules:
  0.0 108.5 jit_solution(16028655514154830567)
XLA Ops:
  0.0 105.2 %evolve_and_rotate.1 = (f32[2,1024,512]{2,1,0:T(8,128)S(1)}, f32[6,8,128]{2,1,0:T(8,128)S(1)}) custom-call(f32[2,1024,512]{2,1,0:T(8,128)} %x.1, s32[8,1,128]{2,1,0:T(1,128)} %bitcast.1, f32[13]{0:T(128)} %coupling_first.1, f32[13]{0:T(128)} %coupling_second.1, f32[16]{0:T(128)} %frozen_coupling.1, s32[16]{0:T(128)} %frozen_bits.1, s32[13]{0:T(128)} %drive_bits.1, ...), custom_call_target="tpu_custom_call" | custom-call | tf_op jit(solution)/shard_map/evolve_and_rotate/pallas_call | solution.py:520
  105.2 3.3 %rotate_last.1 = f32[2,1024,512]{2,1,0:T(8,128)} custom-call(f32[2,1024,512]{2,1,0:T(8,128)S(1)} %get-tuple-element.7.back, f32[6,8,128]{2,1,0:T(8,128)S(1)} %get-tuple-element.8.rot), custom_call_target="tpu_custom_call" | custom-call | tf_op jit(solution)/shard_map/rotate_last/pallas_call | solution.py:581

commit v3 on v1

--- a/solution.py
+++ b/solution.py
@@ -32,6 +32,9 @@
 SIDE = HALO * FB
 LANE_BITS = (0, 1, 2, 3, 10, 11, 12)
 AHEAD = 2
+COL_TILES = COLS // 128
+HALVES = GROUP // 8
+LAST = CHUNKS - 1
 
 
 def bessel_first(term_order, argument):
@@ -125,10 +128,9 @@
     return ladder_first * first / total_first, ladder_second * second / total_second
 
 
-def butterfly(real, imag, rot, bits):
+def butterfly(real, imag, bits):
     count = len(real)
-    for place, bit in enumerate(bits):
-        cosine, driven, kept = rot[3 * bit], rot[3 * bit + 1], rot[3 * bit + 2]
+    for place, (cosine, driven, kept) in bits:
         step = 1 << place
         for low in range(count):
             if low & step:
@@ -151,7 +153,9 @@
     frozen_bits,
     drive_bits,
     angles,
-    out,
+    back,
+    landed,
+    coef_out,
     inb,
     cut_all,
     left,
@@ -172,7 +176,6 @@
     mix_hi,
     mix_lo,
     outb,
-    back,
     in_send,
     in_recv,
     cut_send,
@@ -181,7 +184,8 @@
     halo_recv,
     out_send,
     out_recv,
-    store_sem,
+    tail_send,
+    tail_recv,
 ):
     s = lax.axis_index("spin")
     f = lax.axis_index("fock")
@@ -240,7 +244,7 @@
     def out_copy(i, k):
         p = (s + k) % PLACES
         src = outb.at[i, :, pl.ds(pl.multiple_of(p * GROUP, GROUP), GROUP), :]
-        dst = back.at[:, pl.ds(pl.multiple_of((s * CHUNKS + i) * GROUP, GROUP), GROUP), :]
+        dst = back.at[:, s * CHUNKS + i]
         if k == 0:
             return pltpu.make_async_copy(src, dst, out_recv.at[i, 0])
         return pltpu.make_async_remote_copy(
@@ -248,6 +252,21 @@
             dst_ref=dst,
             send_sem=out_send.at[i, k],
             recv_sem=out_recv.at[i, k],
+            device_id=(p, f),
+            device_id_type=MESH_ID,
+        )
+
+    def tail_copy(h, k):
+        p = (s + k) % PLACES
+        src = outb.at[LAST, :, pl.ds(pl.multiple_of(p * GROUP + h * 8, 8), 8), :]
+        dst = landed.at[:, pl.ds(pl.multiple_of(s * GROUP + h * 8, 8), 8), :]
+        if k == 0:
+            return pltpu.make_async_copy(src, dst, tail_recv.at[h, 0])
+        return pltpu.make_async_remote_copy(
+            src_ref=src,
+            dst_ref=dst,
+            send_sem=tail_send.at[h, k],
+            recv_sem=tail_recv.at[h, k],
             device_id=(p, f),
             device_id_type=MESH_ID,
         )
@@ -331,10 +350,6 @@
         lax.fori_loop(0, groups, group, 0)
 
     def chunk(i, carry):
-        @pl.when(i < CHUNKS - AHEAD)
-        def _():
-            forward(i + AHEAD)
-
         strength_first, strength_second = strengths(
             i, s, coupling_first, coupling_second, frozen_coupling, frozen_bits
         )
@@ -397,74 +412,170 @@
         )
         outb[i, 0] = mixed[:LANES]
         outb[i, 1] = mixed[LANES:]
-        for k in order:
-            out_copy(i, k).start()
+
+        @pl.when(i < LAST)
+        def _():
+            for k in order:
+                out_copy(i, k).start()
+
+        @pl.when(i == LAST)
+        def _():
+            for h in range(HALVES):
+                for k in order:
+                    tail_copy(h, k).start()
+
+        @pl.when(i < CHUNKS - AHEAD)
+        def _():
+            forward(i + AHEAD)
+
         return carry
 
     lax.fori_loop(0, CHUNKS, chunk, 0)
+
+    def turn(bit):
+        return rot[3 * bit], rot[3 * bit + 1], rot[3 * bit + 2]
+
+    for place in range(9):
+        coef_out[2 * CHUNKS + place] = rot[21 + place]
+    for i in range(CHUNKS):
+        real = jnp.ones((8, 128), jnp.float32)
+        imag = jnp.zeros((8, 128), jnp.float32)
+        for place in range(3):
+            cosine, driven, kept = turn(4 + place)
+            if (i >> place) & 1:
+                real, imag = real * cosine, imag * cosine
+            else:
+                real, imag = imag * kept - real * driven, -real * kept - imag * driven
+        coef_out[i] = real
+        coef_out[CHUNKS + i] = imag
+
+    def spot(q, i, half, col):
+        return (
+            q * CHUNKS + i,
+            pl.ds(pl.multiple_of(half * 8, 8), 8),
+            pl.ds(pl.multiple_of(col * 128, 128), 128),
+        )
 
     def rotate_places(i, carry):
         for k in range(PLACES):
             wait_arrival(out_copy(i, k), k)
 
         def unit(u, c):
-            half, col = u // 4, u % 4
-
-            def spot(q):
-                row = pl.multiple_of((q * CHUNKS + i) * GROUP + half * 8, 8)
-                return pl.ds(row, 8), pl.ds(pl.multiple_of(col * 128, 128), 128)
-
-            real = [back[0, spot(q)[0], spot(q)[1]] for q in range(PLACES)]
-            imag = [back[1, spot(q)[0], spot(q)[1]] for q in range(PLACES)]
-            real, imag = butterfly(real, imag, rot, (7, 8, 9))
-            for q in range(PLACES):
-                back[0, spot(q)[0], spot(q)[1]] = real[q]
-                back[1, spot(q)[0], spot(q)[1]] = imag[q]
+            half, col = u // COL_TILES, u % COL_TILES
+            spots = [spot(q, i, half, col) for q in range(PLACES)]
+            real = [back[0, g, r, l] for g, r, l in spots]
+            imag = [back[1, g, r, l] for g, r, l in spots]
+            real, imag = butterfly(real, imag, [(place, turn(7 + place)) for place in range(3)])
+            for q, (g, r, l) in enumerate(spots):
+                back[0, g, r, l] = real[q]
+                back[1, g, r, l] = imag[q]
             return c
 
-        lax.fori_loop(0, 8, unit, 0)
-        return carry
-
-    lax.fori_loop(0, CHUNKS, rotate_places, 0)
-
-    def store_copy(q):
-        rows = pl.ds(pl.multiple_of(q * 128, 128), 128)
-        return pltpu.make_async_copy(back.at[:, rows, :], out.at[:, rows, :], store_sem.at[q])
+        lax.fori_loop(0, 2 * COL_TILES, unit, 0)
+        return carry
+
+    lax.fori_loop(0, LAST, rotate_places, 0)
 
     def rotate_chunks(q, carry):
         def unit(u, c):
-            half, col = u // 4, u % 4
-
-            def spot(i):
-                row = pl.multiple_of((q * CHUNKS + i) * GROUP + half * 8, 8)
-                return pl.ds(row, 8), pl.ds(pl.multiple_of(col * 128, 128), 128)
-
-            real = [back[0, spot(i)[0], spot(i)[1]] for i in range(CHUNKS)]
-            imag = [back[1, spot(i)[0], spot(i)[1]] for i in range(CHUNKS)]
-            real, imag = butterfly(real, imag, rot, (4, 5, 6))
-            for i in range(CHUNKS):
-                back[0, spot(i)[0], spot(i)[1]] = real[i]
-                back[1, spot(i)[0], spot(i)[1]] = imag[i]
+            half, col = u // COL_TILES, u % COL_TILES
+            spots = [spot(q, i, half, col) for i in range(CHUNKS)]
+            zero = jnp.zeros((8, 128), jnp.float32)
+            real = [back[0, g, r, l] for g, r, l in spots[:LAST]] + [zero]
+            imag = [back[1, g, r, l] for g, r, l in spots[:LAST]] + [zero]
+            real, imag = butterfly(real, imag, [(place, turn(4 + place)) for place in range(3)])
+            for i, (g, r, l) in enumerate(spots):
+                back[0, g, r, l] = real[i]
+                back[1, g, r, l] = imag[i]
             return c
 
-        lax.fori_loop(0, 8, unit, 0)
-        store_copy(q).start()
+        lax.fori_loop(0, 2 * COL_TILES, unit, 0)
         return carry
 
     lax.fori_loop(0, PLACES, rotate_chunks, 0)
 
-    def finish(i, carry):
+    def drain(i, carry):
         for k in range(1, PLACES):
             in_copy(i, k).wait_send()
-            out_copy(i, k).wait_send()
         halo_copy(i, 0).wait_send()
         halo_copy(i, 1).wait_send()
-        store_copy(i).wait()
-        return carry
-
-    lax.fori_loop(0, CHUNKS, finish, 0)
+
+        @pl.when(i < LAST)
+        def _():
+            for k in range(1, PLACES):
+                out_copy(i, k).wait_send()
+
+        return carry
+
+    lax.fori_loop(0, CHUNKS, drain, 0)
     for k in range(1, PLACES):
         cut_copy(k).wait_send()
+
+    for h in range(HALVES):
+        for k in range(PLACES):
+            wait_arrival(tail_copy(h, k), k)
+        if h < HALVES - 1:
+
+            def finish(col, carry):
+                finish_tile(landed, back, back, coef_out, h, h, col)
+                return carry
+
+            lax.fori_loop(0, COL_TILES, finish, 0)
+    for h in range(HALVES):
+        for k in range(1, PLACES):
+            tail_copy(h, k).wait_send()
+
+
+def finish_tile(landed, partial, done, coef, half, target, col):
+    cols = pl.ds(pl.multiple_of(col * 128, 128), 128)
+    rows = [pl.ds(q * GROUP + half * 8, 8) for q in range(PLACES)]
+    real = [landed[0, r, cols] for r in rows]
+    imag = [landed[1, r, cols] for r in rows]
+    base = 2 * CHUNKS
+    turns = [(place, tuple(coef[base + 3 * place + e] for e in range(3))) for place in range(3)]
+    real, imag = butterfly(real, imag, turns)
+    source, place = pl.ds(half * 8, 8), pl.ds(target * 8, 8)
+    for i in range(CHUNKS):
+        k_real, k_imag = coef[i], coef[CHUNKS + i]
+        for q in range(PLACES):
+            g = q * CHUNKS + i
+            new_real = partial[0, g, source, cols] + (k_real * real[q] - k_imag * imag[q])
+            new_imag = partial[1, g, source, cols] + (k_real * imag[q] + k_imag * real[q])
+            done[0, g, place, cols] = new_real
+            done[1, g, place, cols] = new_imag
+
+
+def last_kernel(back, landed, coef, out, done, ready_sems, sems):
+    ready = (HALVES - 1) * 8
+    parts = []
+    for j in range(4):
+        groups = pl.ds(j * 16, 16)
+        parts.append(
+            pltpu.make_async_copy(
+                back.at[:, groups, pl.ds(0, ready), :],
+                out.at[:, groups, pl.ds(0, ready), :],
+                ready_sems.at[j],
+            )
+        )
+    for part in parts:
+        part.start()
+
+    def store_copy(col):
+        cols = pl.ds(pl.multiple_of(col * 128, 128), 128)
+        return pltpu.make_async_copy(
+            done.at[:, :, :, cols], out.at[:, :, pl.ds(ready, 8), cols], sems.at[col]
+        )
+
+    def finish(col, carry):
+        finish_tile(landed, back, done, coef, HALVES - 1, 0, col)
+        store_copy(col).start()
+        return carry
+
+    lax.fori_loop(0, COL_TILES, finish, 0)
+    for part in parts:
+        part.wait()
+    for col in range(COL_TILES):
+        store_copy(col).wait()
 
 
 def per_device(
@@ -481,10 +592,15 @@
     padded = pltpu.VMEM((PADDED * FB, LANES), f32)
     dma = pltpu.SemaphoreType.DMA
     smem = pl.BlockSpec(memory_space=pltpu.SMEM)
-    return pl.pallas_call(
+    vmem = pl.BlockSpec(memory_space=pltpu.VMEM)
+    back, landed, coef = pl.pallas_call(
         kernel,
         name="evolve_and_rotate",
-        out_shape=jax.ShapeDtypeStruct(amplitudes.shape, f32),
+        out_shape=[
+            pltpu.VMEM((2, PLACES * CHUNKS, GROUP, COLS), f32),
+            pltpu.VMEM((2, LANES, COLS), f32),
+            pltpu.VMEM((2 * CHUNKS + 9, 8, 128), f32),
+        ],
         in_specs=[
             pl.BlockSpec(memory_space=pl.ANY),
             pl.BlockSpec(memory_space=pltpu.VMEM),
@@ -495,7 +611,7 @@
             smem,
             smem,
         ],
-        out_specs=pl.BlockSpec(memory_space=pl.ANY),
+        out_specs=[vmem, vmem, vmem],
         scratch_shapes=[
             pltpu.VMEM((CHUNKS, 2, LANES, COLS), f32),
             pltpu.VMEM((PLACES, 1, 128), jnp.int32),
@@ -517,7 +633,6 @@
             pltpu.VMEM((2 * LANES, 2 * LANES), jnp.bfloat16),
             pltpu.VMEM((2 * LANES, 2 * LANES), jnp.bfloat16),
             pltpu.VMEM((CHUNKS, 2, LANES, COLS), f32),
-            pltpu.VMEM((2, CHUNKS * LANES, COLS), f32),
             dma((CHUNKS, PLACES)),
             dma((CHUNKS, PLACES)),
             dma((PLACES,)),
@@ -526,10 +641,11 @@
             dma((CHUNKS, 2)),
             dma((CHUNKS, PLACES)),
             dma((CHUNKS, PLACES)),
-            dma((PLACES,)),
+            dma((HALVES, PLACES)),
+            dma((HALVES, PLACES)),
         ],
         compiler_params=pltpu.CompilerParams(
-            collective_id=0, has_side_effects=True, vmem_limit_bytes=60 << 20
+            collective_id=0, has_side_effects=True, vmem_limit_bytes=62_000_000
         ),
     )(
         amplitudes,
@@ -541,6 +657,20 @@
         drive_bits,
         angles,
     )
+    rotated = pl.pallas_call(
+        last_kernel,
+        name="rotate_last",
+        out_shape=jax.ShapeDtypeStruct((2, PLACES * CHUNKS, GROUP, COLS), f32),
+        in_specs=[vmem, vmem, vmem],
+        out_specs=pl.BlockSpec(memory_space=pl.ANY),
+        scratch_shapes=[
+            pltpu.VMEM((2, PLACES * CHUNKS, 8, COLS), f32),
+            dma((4,)),
+            dma((COL_TILES,)),
+        ],
+        compiler_params=pltpu.CompilerParams(vmem_limit_bytes=16 << 20),
+    )(back, landed, coef)
+    return rotated.reshape(amplitudes.shape)
 
 
 def solution(mesh):

time: 113 us -> 107 us (0.947)
  local copies, waits for them, and re-layouts: 4.64 us -> 0 us
  Pallas kernels: 108 us -> 106 us
    unnamed x1 -> x0, local copies, waits for them, and re-layouts: 4.64 us -> none
    pallas_call x1 -> x2, Pallas kernels: 108 us -> 106 us  [the longest x1 104 us: per_device(): pl.pallas_call(kernel, name='evolve_and_rotate', out_shape=[pltpu.VMEM((2...]
where the time goes in v3:
time: 107 us
  Pallas kernels  106 us (99%)
    pallas_call x1, Pallas kernels, per_device(): pl.pallas_call(kernel, name='evolve_and_rotate', out_shape=[pltpu.VMEM((2...  104 us

profile of v3, /device:TPU:1, one launch (start us, length us, event | category | flops | bytes accessed | tf_op | source)
XLA Modules:
  0.0 106.5 jit_solution(1312267672111389237)
XLA Ops:
  0.0 104.4 %evolve_and_rotate.1 = (f32[2,64,16,512]{3,2,1,0:T(8,128)S(1)}, f32[2,128,512]{2,1,0:T(8,128)S(1)}, f32[25,8,128]{2,1,0:T(8,128)S(1)}) custom-call(f32[2,1024,512]{2,1,0:T(8,128)} %x.1, s32[8,1,128]{2,1,0:T(1,128)} %bitcast.2, f32[13]{0:T(128)} %coupling_first.1, f32[13]{0:T(128)} %coupling_second.1, f32[16]{0:T(128)} %frozen_coupling.1, s32[16]{0:T(128)} %frozen_bits.1, ...), custom_call_target="tpu_custom_call" | custom-call | tf_op jit(solution)/shard_map/evolve_and_rotate/pallas_call | solution.py:596
  104.4 2.1 %rotate_last.1 = f32[2,64,16,512]{3,2,1,0:T(8,128)} custom-call(f32[2,64,16,512]{3,2,1,0:T(8,128)S(1)} %get-tuple-element.8.back, f32[2,128,512]{2,1,0:T(8,128)S(1)} %get-tuple-element.9.landed, f32[25,8,128]{2,1,0:T(8,128)S(1)} %get-tuple-element.10.coef), custom_call_target="tpu_custom_call" | custom-call | tf_op jit(solution)/shard_map/rotate_last/pallas_call | solution.py:660

commit v4 on v3

--- a/solution.py
+++ b/solution.py
@@ -202,12 +202,12 @@
     def cut_copy(k):
         p = (s + k) % PLACES
         if k == 0:
-            return pltpu.make_async_copy(cutoffs.at[s], cut_all.at[s], cut_recv.at[0])
+            return pltpu.make_async_copy(cutoffs.at[s], cut_all.at[s], cut_recv)
         return pltpu.make_async_remote_copy(
             src_ref=cutoffs.at[p],
             dst_ref=cut_all.at[s],
-            send_sem=cut_send.at[k],
-            recv_sem=cut_recv.at[k],
+            send_sem=cut_send,
+            recv_sem=cut_recv,
             device_id=(p, f),
             device_id_type=MESH_ID,
         )
@@ -217,12 +217,12 @@
         src = x.at[:, pl.ds(pl.multiple_of((p * CHUNKS + i) * GROUP, GROUP), GROUP), :]
         dst = inb.at[i, :, pl.ds(pl.multiple_of(s * GROUP, GROUP), GROUP), :]
         if k == 0:
-            return pltpu.make_async_copy(src, dst, in_recv.at[i, 0])
+            return pltpu.make_async_copy(src, dst, in_recv.at[i])
         return pltpu.make_async_remote_copy(
             src_ref=src,
             dst_ref=dst,
-            send_sem=in_send.at[i, k],
-            recv_sem=in_recv.at[i, k],
+            send_sem=in_send,
+            recv_sem=in_recv.at[i],
             device_id=(p, f),
             device_id_type=MESH_ID,
         )
@@ -235,8 +235,8 @@
         return pltpu.make_async_remote_copy(
             src_ref=src,
             dst_ref=dst,
-            send_sem=halo_send.at[i, side],
-            recv_sem=halo_recv.at[i, side],
+            send_sem=halo_send,
+            recv_sem=halo_recv.at[i],
             device_id=(s, near),
             device_id_type=MESH_ID,
         )
@@ -246,12 +246,12 @@
         src = outb.at[i, :, pl.ds(pl.multiple_of(p * GROUP, GROUP), GROUP), :]
         dst = back.at[:, s * CHUNKS + i]
         if k == 0:
-            return pltpu.make_async_copy(src, dst, out_recv.at[i, 0])
+            return pltpu.make_async_copy(src, dst, out_recv.at[i])
         return pltpu.make_async_remote_copy(
             src_ref=src,
             dst_ref=dst,
-            send_sem=out_send.at[i, k],
-            recv_sem=out_recv.at[i, k],
+            send_sem=out_send,
+            recv_sem=out_recv.at[i],
             device_id=(p, f),
             device_id_type=MESH_ID,
         )
@@ -261,21 +261,20 @@
         src = outb.at[LAST, :, pl.ds(pl.multiple_of(p * GROUP + h * 8, 8), 8), :]
         dst = landed.at[:, pl.ds(pl.multiple_of(s * GROUP + h * 8, 8), 8), :]
         if k == 0:
-            return pltpu.make_async_copy(src, dst, tail_recv.at[h, 0])
+            return pltpu.make_async_copy(src, dst, tail_recv.at[h])
         return pltpu.make_async_remote_copy(
             src_ref=src,
             dst_ref=dst,
-            send_sem=tail_send.at[h, k],
-            recv_sem=tail_recv.at[h, k],
+            send_sem=tail_send,
+            recv_sem=tail_recv.at[h],
             device_id=(p, f),
             device_id_type=MESH_ID,
         )
 
-    def wait_arrival(copy, k):
-        if k == 0:
-            copy.wait()
-        else:
-            copy.wait_recv()
+    def wait_for(sem, like):
+        pltpu.make_async_copy(like, like, sem).wait()
+
+    others = pl.ds(0, LANES - GROUP)
 
     order = (4, 3, 5, 2, 6, 1, 7, 0)
     for k in order:
@@ -291,12 +290,10 @@
     fill_rotations(angles, drive_bits, rot)
     fill_mixer(rot, mix_hi, mix_lo)
     fill_diagonal(f, diag)
-    for k in range(PLACES):
-        wait_arrival(cut_copy(k), k)
+    wait_for(cut_recv, cut_all)
 
     def forward(i):
-        for k in range(PLACES):
-            wait_arrival(in_copy(i, k), k)
+        wait_for(in_recv.at[i], inb.at[i])
         halo_copy(i, 0).start()
         halo_copy(i, 1).start()
 
@@ -371,8 +368,7 @@
         low_side = double * jnp.sqrt(2.0 * sub / FB)
         high_side = jnp.where(sub < 7.0, double * jnp.sqrt((2.0 * sub + 2.0) / FB), 0.0)
 
-        halo_copy(i, 0).wait_recv()
-        halo_copy(i, 1).wait_recv()
+        wait_for(halo_recv.at[i], inb.at[i])
 
         for part, natural in ((0, nat_re), (1, nat_im)):
             for b in range(8):
@@ -457,8 +453,7 @@
         )
 
     def rotate_places(i, carry):
-        for k in range(PLACES):
-            wait_arrival(out_copy(i, k), k)
+        wait_for(out_recv.at[i], inb.at[i])
 
         def unit(u, c):
             half, col = u // COL_TILES, u % COL_TILES
@@ -494,26 +489,13 @@
 
     lax.fori_loop(0, PLACES, rotate_chunks, 0)
 
-    def drain(i, carry):
-        for k in range(1, PLACES):
-            in_copy(i, k).wait_send()
-        halo_copy(i, 0).wait_send()
-        halo_copy(i, 1).wait_send()
-
-        @pl.when(i < LAST)
-        def _():
-            for k in range(1, PLACES):
-                out_copy(i, k).wait_send()
-
-        return carry
-
-    lax.fori_loop(0, CHUNKS, drain, 0)
-    for k in range(1, PLACES):
-        cut_copy(k).wait_send()
+    wait_for(cut_send, cut_all.at[pl.ds(0, PLACES - 1)])
+    wait_for(in_send, inb.at[:, :, others, :])
+    wait_for(halo_send, inb)
+    wait_for(out_send, inb.at[pl.ds(0, LAST), :, others, :])
 
     for h in range(HALVES):
-        for k in range(PLACES):
-            wait_arrival(tail_copy(h, k), k)
+        wait_for(tail_recv.at[h], landed.at[:, pl.ds(0, LANES // HALVES), :])
         if h < HALVES - 1:
 
             def finish(col, carry):
@@ -521,9 +503,7 @@
                 return carry
 
             lax.fori_loop(0, COL_TILES, finish, 0)
-    for h in range(HALVES):
-        for k in range(1, PLACES):
-            tail_copy(h, k).wait_send()
+    wait_for(tail_send, landed.at[:, others, :])
 
 
 def finish_tile(landed, partial, done, coef, half, target, col):
@@ -545,7 +525,7 @@
             done[1, g, place, cols] = new_imag
 
 
-def last_kernel(back, landed, coef, out, done, ready_sems, sems):
+def last_kernel(back, landed, coef, out, done, ready_sem, done_sem):
     ready = (HALVES - 1) * 8
     parts = []
     for j in range(4):
@@ -554,7 +534,7 @@
             pltpu.make_async_copy(
                 back.at[:, groups, pl.ds(0, ready), :],
                 out.at[:, groups, pl.ds(0, ready), :],
-                ready_sems.at[j],
+                ready_sem,
             )
         )
     for part in parts:
@@ -563,7 +543,7 @@
     def store_copy(col):
         cols = pl.ds(pl.multiple_of(col * 128, 128), 128)
         return pltpu.make_async_copy(
-            done.at[:, :, :, cols], out.at[:, :, pl.ds(ready, 8), cols], sems.at[col]
+            done.at[:, :, :, cols], out.at[:, :, pl.ds(ready, 8), cols], done_sem
         )
 
     def finish(col, carry):
@@ -572,10 +552,9 @@
         return carry
 
     lax.fori_loop(0, COL_TILES, finish, 0)
-    for part in parts:
-        part.wait()
-    for col in range(COL_TILES):
-        store_copy(col).wait()
+    first = back.at[:, :, pl.ds(0, ready), :]
+    pltpu.make_async_copy(first, first, ready_sem).wait()
+    pltpu.make_async_copy(done, done, done_sem).wait()
 
 
 def per_device(
@@ -633,16 +612,16 @@
             pltpu.VMEM((2 * LANES, 2 * LANES), jnp.bfloat16),
             pltpu.VMEM((2 * LANES, 2 * LANES), jnp.bfloat16),
             pltpu.VMEM((CHUNKS, 2, LANES, COLS), f32),
-            dma((CHUNKS, PLACES)),
-            dma((CHUNKS, PLACES)),
-            dma((PLACES,)),
-            dma((PLACES,)),
-            dma((CHUNKS, 2)),
-            dma((CHUNKS, 2)),
-            dma((CHUNKS, PLACES)),
-            dma((CHUNKS, PLACES)),
-            dma((HALVES, PLACES)),
-            dma((HALVES, PLACES)),
+            dma,
+            dma((CHUNKS,)),
+            dma,
+            dma,
+            dma,
+            dma((CHUNKS,)),
+            dma,
+            dma((LAST,)),
+            dma,
+            dma((HALVES,)),
         ],
         compiler_params=pltpu.CompilerParams(
             collective_id=0, has_side_effects=True, vmem_limit_bytes=62_000_000
@@ -665,8 +644,8 @@
         out_specs=pl.BlockSpec(memory_space=pl.ANY),
         scratch_shapes=[
             pltpu.VMEM((2, PLACES * CHUNKS, 8, COLS), f32),
-            dma((4,)),
-            dma((COL_TILES,)),
+            dma,
+            dma,
         ],
         compiler_params=pltpu.CompilerParams(vmem_limit_bytes=16 << 20),
     )(back, landed, coef)

time: 107 us -> 104 us (0.972)
  Pallas kernels: 106 us -> 104 us
    pallas_call x1, Pallas kernels: 104 us -> 102 us  [per_device(): pl.pallas_call(kernel, name='evolve_and_rotate', out_shape=[pltpu.VMEM((2...]
where the time goes in v4:
time: 104 us
  Pallas kernels  104 us (100%)
    pallas_call x1, Pallas kernels, per_device(): pl.pallas_call(kernel, name='evolve_and_rotate', out_shape=[pltpu.VMEM((2...  102 us

profile of v4, /device:TPU:1, one launch (start us, length us, event | category | flops | bytes accessed | tf_op | source)
XLA Modules:
  0.0 103.7 jit_solution(1389784122895394968)
XLA Ops:
  0.0 101.7 %evolve_and_rotate.1 = (f32[2,64,16,512]{3,2,1,0:T(8,128)S(1)}, f32[2,128,512]{2,1,0:T(8,128)S(1)}, f32[25,8,128]{2,1,0:T(8,128)S(1)}) custom-call(f32[2,1024,512]{2,1,0:T(8,128)} %x.1, s32[8,1,128]{2,1,0:T(1,128)} %bitcast.2, f32[13]{0:T(128)} %coupling_first.1, f32[13]{0:T(128)} %coupling_second.1, f32[16]{0:T(128)} %frozen_coupling.1, s32[16]{0:T(128)} %frozen_bits.1, ...), custom_call_target="tpu_custom_call" | custom-call | tf_op jit(solution)/shard_map/evolve_and_rotate/pallas_call | solution.py:575
  101.7 2.0 %rotate_last.1 = f32[2,64,16,512]{3,2,1,0:T(8,128)} custom-call(f32[2,64,16,512]{3,2,1,0:T(8,128)S(1)} %get-tuple-element.8.back, f32[2,128,512]{2,1,0:T(8,128)S(1)} %get-tuple-element.9.landed, f32[25,8,128]{2,1,0:T(8,128)S(1)} %get-tuple-element.10.coef), custom_call_target="tpu_custom_call" | custom-call | tf_op jit(solution)/shard_map/rotate_last/pallas_call | solution.py:639

commit v5 on v4

--- a/solution.py
+++ b/solution.py
@@ -147,12 +147,12 @@
 def kernel(
     x,
     cutoffs,
-    coupling_first,
-    coupling_second,
-    frozen_coupling,
-    frozen_bits,
-    drive_bits,
-    angles,
+    small_0,
+    small_1,
+    small_2,
+    small_3,
+    small_4,
+    small_5,
     back,
     landed,
     coef_out,
@@ -186,6 +186,13 @@
     out_recv,
     tail_send,
     tail_recv,
+    coupling_first,
+    coupling_second,
+    frozen_coupling,
+    frozen_bits,
+    drive_bits,
+    angles,
+    small_sem,
 ):
     s = lax.axis_index("spin")
     f = lax.axis_index("fock")
@@ -287,6 +294,23 @@
 
     lax.fori_loop(0, CHUNKS, start_in, 0)
 
+    fetches = [
+        pltpu.make_async_copy(src, dst, small_sem.at[j])
+        for j, (src, dst) in enumerate(
+            (
+                (small_5, angles),
+                (small_4, drive_bits),
+                (small_0, coupling_first),
+                (small_1, coupling_second),
+                (small_2, frozen_coupling),
+                (small_3, frozen_bits),
+            )
+        )
+    ]
+    for fetch in fetches:
+        fetch.start()
+    for fetch in fetches:
+        fetch.wait()
     fill_rotations(angles, drive_bits, rot)
     fill_mixer(rot, mix_hi, mix_lo)
     fill_diagonal(f, diag)
@@ -570,7 +594,6 @@
     f32 = jnp.float32
     padded = pltpu.VMEM((PADDED * FB, LANES), f32)
     dma = pltpu.SemaphoreType.DMA
-    smem = pl.BlockSpec(memory_space=pltpu.SMEM)
     vmem = pl.BlockSpec(memory_space=pltpu.VMEM)
     back, landed, coef = pl.pallas_call(
         kernel,
@@ -582,14 +605,8 @@
         ],
         in_specs=[
             pl.BlockSpec(memory_space=pl.ANY),
-            pl.BlockSpec(memory_space=pltpu.VMEM),
-            smem,
-            smem,
-            smem,
-            smem,
-            smem,
-            smem,
-        ],
+        ]
+        * 8,
         out_specs=[vmem, vmem, vmem],
         scratch_shapes=[
             pltpu.VMEM((CHUNKS, 2, LANES, COLS), f32),
@@ -622,9 +639,16 @@
             dma((LAST,)),
             dma,
             dma((HALVES,)),
+            pltpu.SMEM((SPINS,), f32),
+            pltpu.SMEM((SPINS,), f32),
+            pltpu.SMEM((FROZEN,), f32),
+            pltpu.SMEM((FROZEN,), jnp.int32),
+            pltpu.SMEM((SPINS,), jnp.int32),
+            pltpu.SMEM((SPINS,), f32),
+            dma((6,)),
         ],
         compiler_params=pltpu.CompilerParams(
-            collective_id=0, has_side_effects=True, vmem_limit_bytes=62_000_000
+            collective_id=0, has_side_effects=True, vmem_limit_bytes=62_100_000
         ),
     )(
         amplitudes,

time: 104 us -> 103 us (level)
  no operation moved by 1% of the time
where the time goes in v5:
time: 103 us
  Pallas kernels  103 us (100%)
    pallas_call x1, Pallas kernels, per_device(): pl.pallas_call(kernel, name='evolve_and_rotate', out_shape=[pltpu.VMEM((2...  101 us

profile of v5, /device:TPU:1, one launch (start us, length us, event | category | flops | bytes accessed | tf_op | source)
XLA Modules:
  0.0 102.8 jit_solution(10614104623823409607)
XLA Ops:
  0.0 100.7 %evolve_and_rotate.1 = (f32[2,64,16,512]{3,2,1,0:T(8,128)S(1)}, f32[2,128,512]{2,1,0:T(8,128)S(1)}, f32[25,8,128]{2,1,0:T(8,128)S(1)}) custom-call(f32[2,1024,512]{2,1,0:T(8,128)} %x.1, s32[8,1,128]{2,1,0:T(1,128)} %bitcast.2, f32[13]{0:T(128)} %small_0.1, f32[13]{0:T(128)} %small_1.1, f32[16]{0:T(128)} %small_2.1, s32[16]{0:T(128)} %small_3.1, s32[13]{0:T(128)} %small_4.1, ...), custom_call_target="tpu_custom_call" | custom-call | tf_op jit(solution)/shard_map/evolve_and_rotate/pallas_call | solution.py:598
  100.7 2.0 %rotate_last.1 = f32[2,64,16,512]{3,2,1,0:T(8,128)} custom-call(f32[2,64,16,512]{3,2,1,0:T(8,128)S(1)} %get-tuple-element.8.back, f32[2,128,512]{2,1,0:T(8,128)S(1)} %get-tuple-element.9.landed, f32[25,8,128]{2,1,0:T(8,128)S(1)} %get-tuple-element.10.coef), custom_call_target="tpu_custom_call" | custom-call | tf_op jit(solution)/shard_map/rotate_last/pallas_call | solution.py:663

commit v6 on v5

--- a/solution.py
+++ b/solution.py
@@ -32,6 +32,7 @@
 SIDE = HALO * FB
 LANE_BITS = (0, 1, 2, 3, 10, 11, 12)
 AHEAD = 2
+SPARE = 8
 COL_TILES = COLS // 128
 HALVES = GROUP // 8
 LAST = CHUNKS - 1
@@ -418,7 +419,7 @@
         for k in range(DEGREE - 1, -1, -1):
             series_step(k, i, (link, low_side, high_side))
 
-        y = jnp.concatenate([y_re[...], y_im[...]], axis=1)
+        y = jnp.concatenate([y_re[:COLS, :], y_im[:COLS, :]], axis=1)
         y_hi = y.astype(jnp.bfloat16)
         y_lo = (y - y_hi.astype(jnp.float32)).astype(jnp.bfloat16)
 
@@ -613,18 +614,18 @@
             pltpu.VMEM((PLACES, 1, 128), jnp.int32),
             pltpu.VMEM((CHUNKS, 2, LANES, SIDE), f32),
             pltpu.VMEM((CHUNKS, 2, LANES, SIDE), f32),
-            pltpu.VMEM((LEVELS * FB, LANES), f32),
-            pltpu.VMEM((LEVELS * FB, LANES), f32),
+            pltpu.VMEM((LEVELS * FB + SPARE, LANES), f32),
+            pltpu.VMEM((LEVELS * FB + SPARE, LANES), f32),
             padded,
             padded,
             padded,
             padded,
             padded,
             padded,
-            pltpu.VMEM((COLS, LANES), f32),
-            pltpu.VMEM((COLS, LANES), f32),
+            pltpu.VMEM((COLS + SPARE, LANES), f32),
+            pltpu.VMEM((COLS + SPARE, LANES), f32),
             padded,
-            pltpu.VMEM((72, LANES), f32),
+            pltpu.VMEM((72 + SPARE, LANES), f32),
             pltpu.VMEM((3 * SPINS, 8, 128), f32),
             pltpu.VMEM((2 * LANES, 2 * LANES), jnp.bfloat16),
             pltpu.VMEM((2 * LANES, 2 * LANES), jnp.bfloat16),

time: 103 us -> 103 us (level)
  no operation moved by 1% of the time
where the time goes in v6:
time: 103 us
  Pallas kernels  103 us (100%)
    pallas_call x1, Pallas kernels, per_device(): pl.pallas_call(kernel, name='evolve_and_rotate', out_shape=[pltpu.VMEM((2...  101 us

profile of v6, /device:TPU:1, one launch (start us, length us, event | category | flops | bytes accessed | tf_op | source)
XLA Modules:
  0.0 102.8 jit_solution(2929769992015627736)
XLA Ops:
  0.0 100.7 %evolve_and_rotate.1 = (f32[2,64,16,512]{3,2,1,0:T(8,128)S(1)}, f32[2,128,512]{2,1,0:T(8,128)S(1)}, f32[25,8,128]{2,1,0:T(8,128)S(1)}) custom-call(f32[2,1024,512]{2,1,0:T(8,128)} %x.1, s32[8,1,128]{2,1,0:T(1,128)} %bitcast.2, f32[13]{0:T(128)} %small_0.1, f32[13]{0:T(128)} %small_1.1, f32[16]{0:T(128)} %small_2.1, s32[16]{0:T(128)} %small_3.1, s32[13]{0:T(128)} %small_4.1, ...), custom_call_target="tpu_custom_call" | custom-call | tf_op jit(solution)/shard_map/evolve_and_rotate/pallas_call | solution.py:599
  100.7 2.0 %rotate_last.1 = f32[2,64,16,512]{3,2,1,0:T(8,128)} custom-call(f32[2,64,16,512]{3,2,1,0:T(8,128)S(1)} %get-tuple-element.8.back, f32[2,128,512]{2,1,0:T(8,128)S(1)} %get-tuple-element.9.landed, f32[25,8,128]{2,1,0:T(8,128)S(1)} %get-tuple-element.10.coef), custom_call_target="tpu_custom_call" | custom-call | tf_op jit(solution)/shard_map/rotate_last/pallas_call | solution.py:664

commit v7 on v5

--- a/solution.py
+++ b/solution.py
@@ -31,7 +31,7 @@
 COLS = OWN * FB
 SIDE = HALO * FB
 LANE_BITS = (0, 1, 2, 3, 10, 11, 12)
-AHEAD = 2
+AHEAD = 3
 COL_TILES = COLS // 128
 HALVES = GROUP // 8
 LAST = CHUNKS - 1
@@ -200,7 +200,7 @@
     f_right = (f + 1) % 16
 
     barrier = pltpu.get_barrier_semaphore()
-    for k in range(1, PLACES):
+    for k in (4, 3, 5, 2, 6, 7, 1):
         pl.semaphore_signal(barrier, inc=1, device_id=((s + k) % PLACES, f), device_id_type=MESH_ID)
     for near in (f_left, f_right):
         pl.semaphore_signal(barrier, inc=1, device_id=(s, near), device_id_type=MESH_ID)
@@ -284,15 +284,15 @@
     others = pl.ds(0, LANES - GROUP)
 
     order = (4, 3, 5, 2, 6, 1, 7, 0)
-    for k in order:
-        cut_copy(k).start()
-
     def start_in(i, carry):
         for k in order:
             in_copy(i, k).start()
         return carry
 
-    lax.fori_loop(0, CHUNKS, start_in, 0)
+    start_in(0, 0)
+    for k in order:
+        cut_copy(k).start()
+    lax.fori_loop(1, CHUNKS, start_in, 0)
 
     fetches = [
         pltpu.make_async_copy(src, dst, small_sem.at[j])

time: 103 us -> 103 us (level)
  no operation moved by 1% of the time
where the time goes in v7:
time: 103 us
  Pallas kernels  103 us (100%)
    pallas_call x1, Pallas kernels, per_device(): pl.pallas_call(kernel, name='evolve_and_rotate', out_shape=[pltpu.VMEM((2...  101 us

profile of v7, /device:TPU:1, one launch (start us, length us, event | category | flops | bytes accessed | tf_op | source)
XLA Modules:
  0.0 102.8 jit_solution(10412171321365158257)
XLA Ops:
  0.0 100.8 %evolve_and_rotate.1 = (f32[2,64,16,512]{3,2,1,0:T(8,128)S(1)}, f32[2,128,512]{2,1,0:T(8,128)S(1)}, f32[25,8,128]{2,1,0:T(8,128)S(1)}) custom-call(f32[2,1024,512]{2,1,0:T(8,128)} %x.1, s32[8,1,128]{2,1,0:T(1,128)} %bitcast.2, f32[13]{0:T(128)} %small_0.1, f32[13]{0:T(128)} %small_1.1, f32[16]{0:T(128)} %small_2.1, s32[16]{0:T(128)} %small_3.1, s32[13]{0:T(128)} %small_4.1, ...), custom_call_target="tpu_custom_call" | custom-call | tf_op jit(solution)/shard_map/evolve_and_rotate/pallas_call | solution.py:598
  100.8 2.0 %rotate_last.1 = f32[2,64,16,512]{3,2,1,0:T(8,128)} custom-call(f32[2,64,16,512]{3,2,1,0:T(8,128)S(1)} %get-tuple-element.8.back, f32[2,128,512]{2,1,0:T(8,128)S(1)} %get-tuple-element.9.landed, f32[25,8,128]{2,1,0:T(8,128)S(1)} %get-tuple-element.10.coef), custom_call_target="tpu_custom_call" | custom-call | tf_op jit(solution)/shard_map/rotate_last/pallas_call | solution.py:663
